TPU v7x, 256 devices: a whole 4x4x8 slice. The times are simulated.
256 devices in a mesh: pipe: 4 (over x), seq: 64 (over y, z, core).
Axes of the slice: x: 4, y: 4, z: 8, core: 2. Of those that a mesh axis runs over, the one named last changes fastest.
Arguments:
- arriving: bfloat16 [4, 65536, 2048], P('pipe', 'seq'), may hold values from -6 to 6
- loss_grad: bfloat16 [65536, 2048], P('seq', 'pipe'), may hold values from -6 to 6
- first_blocks: bfloat16 [4, 256, 256, 256], P('pipe', 'seq'), may hold values from -0.375 to 0.375
- second_blocks: bfloat16 [4, 256, 256, 256], P('pipe', 'seq'), may hold values from -0.375 to 0.375
- inner_gain: bfloat16 [4, 2048], P('pipe'), may hold values from 0.25 to 1.75
- outer_gain: bfloat16 [4, 2048], P('pipe'), may hold values from 0.25 to 1.75
Outputs:
- entering: bfloat16 [4, 65536, 2048], P('pipe', 'seq')
- leaving: bfloat16 [65536, 2048], P('seq', 'pipe')
All inputs are finite; a program needn't handle non-finite values.
Results may differ from a plain program's by a relative error of at most 0.0059.
Values may be sent and summed in bfloat16 or wider, within the bound.
No kernel may reach another device: no remote copies, remote signals or barrier semaphores. Data moves between devices by JAX's collectives and lax.ppermute only.
A program may use at most 128 MiB of HBM per device.

v0:
```python
import functools

import jax
import jax.numpy as jnp
from jax import lax
from jax.experimental import pallas as pl
from jax.experimental.pallas import tpu as pltpu
from jax.sharding import PartitionSpec as P


F32, BF16 = jnp.float32, jnp.bfloat16


def dot(a, b):
    return lax.dot_general(a, b, (((1,), (0,)), ((), ())), preferred_element_type=F32)


def exchange(rows, devices):
    tile = rows.shape[0] // devices
    blocks = rows.reshape(devices, tile, rows.shape[1])
    blocks = lax.all_to_all(blocks, "seq", split_axis=0, concat_axis=0)
    return blocks.reshape(rows.shape)


def reorder_kernel(count, gain, rows_in, rows_out):
    order = rows_in.shape[0] // count
    chunk, tile = order // count, count * count
    n = lax.broadcasted_iota(jnp.int32, (order, order), 0)
    m = lax.broadcasted_iota(jnp.int32, (order, order), 1)
    place = (m == (n // count % count) * chunk + (n // tile) * count + n % count).astype(BF16)
    for group in range(count):
        starts = [il * order + group * chunk for il in range(count)]
        taken = jnp.concatenate([rows_in[s:s + chunk, :] for s in starts], axis=0)
        if gain is not None:
            taken = (taken.astype(F32) * gain[...]).astype(BF16)
        rows_out[group * order:(group + 1) * order, :] = dot(place, taken).astype(BF16)


def reorder(rows_in, count, gain=None):
    rows, channels = rows_in.shape
    width = min(1024, channels)
    specs = [pl.BlockSpec((rows, width), lambda n: (0, n))]
    operands = [rows_in]
    kernel = functools.partial(reorder_kernel, count, None)
    if gain is not None:
        specs.insert(0, pl.BlockSpec((1, width), lambda n: (0, n)))
        operands.insert(0, gain)
        kernel = functools.partial(reorder_kernel, count)
    return pl.pallas_call(
        kernel,
        out_shape=jax.ShapeDtypeStruct(rows_in.shape, BF16),
        grid=(channels // width,),
        in_specs=specs,
        out_specs=pl.BlockSpec((rows, width), lambda n: (0, n)),
        cost_estimate=pl.CostEstimate(
            flops=2 * rows * (rows // count) * channels, bytes_accessed=4 * rows * channels, transcendentals=0
        ),
    )(*operands)


def scale_kernel(flag, gain, here, moved, *rest):
    gradient = jnp.where(flag[0] == 1, here[...].astype(F32), moved[...].astype(F32))
    rest[-1][...] = (gradient * gain[...]).astype(BF16)


def scale_into(flag, gain, here, moved, total, at, buffer=None):
    rows, width = here.shape
    step, column = rows // 4, at // width
    block = pl.BlockSpec((step, width), lambda n: (n, 0))
    in_specs = [
        pl.BlockSpec(memory_space=pltpu.SMEM),
        pl.BlockSpec((1, width), lambda n: (0, 0)),
        block,
        block,
    ]
    operands = [flag, gain, here, moved]
    aliases = {}
    if buffer is not None:
        in_specs.append(pl.BlockSpec(memory_space=pl.ANY))
        operands.append(buffer)
        aliases = {4: 0}
    return pl.pallas_call(
        scale_kernel,
        out_shape=jax.ShapeDtypeStruct((rows, total), BF16),
        grid=(4,),
        in_specs=in_specs,
        out_specs=pl.BlockSpec((step, width), lambda n: (n, column)),
        input_output_aliases=aliases,
        cost_estimate=pl.CostEstimate(flops=rows * width, bytes_accessed=6 * rows * width, transcendentals=0),
    )(*operands)


def product_kernel(weights, columns, *rest):
    rest[-1][...] = dot(weights[...], columns[...]).astype(BF16)


def product_into(weights, columns, total, at, buffer=None):
    rows, depth = weights.shape
    width = min(512, columns.shape[1])
    steps, first = columns.shape[1] // width, at // width
    in_specs = [
        pl.BlockSpec((rows, depth), lambda n: (0, 0), pipeline_mode=pl.Buffered(1)),
        pl.BlockSpec((depth, width), lambda n: (0, n)),
    ]
    operands = [weights, columns]
    aliases = {}
    if buffer is not None:
        in_specs.append(pl.BlockSpec(memory_space=pl.ANY))
        operands.append(buffer)
        aliases = {2: 0}
    return pl.pallas_call(
        product_kernel,
        out_shape=jax.ShapeDtypeStruct((rows, total), BF16),
        grid=(steps,),
        in_specs=in_specs,
        out_specs=pl.BlockSpec((rows, width), lambda n: (0, first + n)),
        input_output_aliases=aliases,
        cost_estimate=pl.CostEstimate(
            flops=2 * rows * depth * columns.shape[1],
            bytes_accessed=2 * (rows * depth + 2 * rows * columns.shape[1]),
            transcendentals=0,
        ),
    )(*operands)


def local_program(arriving, loss_grad, first_blocks, second_blocks, inner_gain, outer_gain):
    sections = lax.axis_size("pipe")
    devices = lax.axis_size("seq")
    position = lax.axis_index("pipe")
    last = sections - 1
    first, second = first_blocks[0], second_blocks[0]
    count, order = first.shape[0], first.shape[1]
    rows, channels = arriving.shape[1:]
    piece = loss_grad.shape[1]
    tile = count * count

    out = lax.broadcasted_iota(jnp.int32, (rows, rows), 0)
    into = lax.broadcasted_iota(jnp.int32, (rows, rows), 1)
    natural = (out // count % count) * order + (out // tile) * count + out % count

    at = lax.broadcasted_iota(jnp.int32, (count, rows, order), 1)
    col = lax.broadcasted_iota(jnp.int32, (count, rows, order), 2)
    own = lax.broadcasted_iota(jnp.int32, (count, rows, order), 0)
    place = (at == col * count + own).astype(BF16)
    tall = jnp.einsum("jni,jki->nk", place, second, preferred_element_type=F32).astype(BF16)
    k = lax.broadcasted_iota(jnp.int32, (order, rows), 0)
    r = lax.broadcasted_iota(jnp.int32, (order, rows), 1)
    wide = dot(tall, (k == r // count).astype(BF16))
    second_spread = jnp.where(out % count == into % count, wide, 0.0).astype(BF16)

    pick = (k == (r // tile) * count + r % count).astype(BF16)
    wide = jnp.einsum("ikj,kr->ijr", first, pick, preferred_element_type=F32).reshape(rows, rows)
    first_spread = jnp.where(out // order == into // count % count, wide, 0.0).astype(BF16)

    inner, outer = inner_gain.astype(F32), outer_gain.astype(F32)
    restore = (natural.T == into.T).astype(BF16)
    first_sent = reorder(first_spread, count)

    def mix(columns):
        return dot(second_spread, columns).astype(BF16)

    def finish(gradient, weights, returned, cols):
        spread = dot(weights, returned)
        return (gradient.astype(F32) + outer[:, cols] * spread).astype(BF16)

    whole = slice(0, channels)
    halves = (slice(0, channels // 2), slice(channels // 2, channels))
    pieces = [slice(q * piece, (q + 1) * piece) for q in range(sections)]
    per_half = sections // 2

    first_sending = exchange(reorder(arriving[0], count, inner), devices)

    reordered = reorder(arriving[0], count)
    loss_sent = reorder(loss_grad, count)
    lost = [loss_sent if q == last else lax.ppermute(loss_sent, "pipe", [(q, last)]) for q in range(sections)]
    columns, lost, first_sent, reordered = lax.optimization_barrier((first_sending, lost, first_sent, reordered))

    back = [(i + 1, i) for i in range(sections - 1)]
    returned = [exchange(mix(columns[:, h]), devices) for h in halves]
    flag = (position == last).astype(jnp.int32).reshape(1)

    def step(q):
        cut = slice(q % per_half * piece, (q % per_half + 1) * piece)
        result = finish(reordered[:, pieces[q]], first_sent, returned[q // per_half][:, cut], pieces[q])
        return result, lax.ppermute(result, "pipe", back)

    def fill(buffer, q):
        at = q % per_half * piece
        return scale_into(flag, inner[:, pieces[q]], lost[q], moved[q], channels // 2, at, buffer)

    passed, moved, sent = [None] * sections, [None] * sections, []
    for q in range(per_half):
        passed[q], moved[q] = step(q)
    buffer = None
    for q in range(per_half):
        buffer = fill(buffer, q)
    passed[per_half], moved[per_half] = step(per_half)
    buffer, passed[per_half] = lax.optimization_barrier((buffer, passed[per_half]))
    sent.append(exchange(buffer, devices))
    for q in range(per_half + 1, sections):
        passed[q], moved[q] = step(q)
    buffer = None
    for q in range(per_half, sections):
        buffer = fill(buffer, q)
    sent.append(exchange(buffer, devices))

    leaving = passed[0]
    for q in range(1, sections):
        leaving = jnp.where(position == q, lax.ppermute(passed[q], "pipe", [(0, q)]), leaving)
    leaving = dot(restore, leaving).astype(BF16)

    mixed = product_into(second_spread, sent[0], channels, 0)
    mixed = product_into(second_spread, sent[1], channels, channels // 2, mixed)
    final = exchange(mixed, devices)
    source = jnp.concatenate([jnp.where(position == last, a, b) for a, b in zip(lost, moved)], axis=1)
    source = dot(restore, source).astype(BF16)
    final, source, leaving = lax.optimization_barrier((final, source, leaving))
    entering = finish(source, first_spread, final, whole)
    return entering[None], leaving


def solution(mesh):
    placed = (
        P("pipe", "seq", None),
        P("seq", "pipe"),
        P("pipe", "seq", None, None),
        P("pipe", "seq", None, None),
        P("pipe", None),
        P("pipe", None),
    )
    return jax.shard_map(
        local_program,
        mesh=mesh,
        in_specs=placed,
        out_specs=(P("pipe", "seq", None), P("seq", "pipe")),
        check_vma=False,
    )
```

profile of v0, /device:TPU:1, one launch (start us, length us, event | category | flops | bytes accessed | tf_op | source)
XLA Modules:
  0.0 486.7 jit_solution(5280159981124351168)
XLA Ops:
  2.0 4.6 shard_map.77
  6.6 13.3 %all-to-all-start = ((bf16[64,16,2048]{2,1,0:T(8,128)(2,1)}), bf16[64,16,2048]{2,1,0:T(8,128)(2,1)}, u32[]{:S(2)}, u32[]{:S(2)}) async-start(bf16[64,16,2048]{2,1,0:T(8,128)(2,1)} %bitcast.56), calls=%async_computation | async-start | bytes 8388608 | tf_op jit(solution)/shard_map/all_to_all | solution.py:21
  25.9 4.7 collective-permute-start
  44.4 29.9 %collective-permute-done.here = bf16[1024,512]{1,0:T(8,128)(2,1)} collective-permute-done((bf16[1024,512]{1,0:T(8,128)(2,1)}, bf16[1024,512]{1,0:T(8,128)(2,1)}, u32[]{:S(2)}, u32[]{:S(2)}) %collective-permute-start) | collective-permute-done | bytes 1048608 | tf_op jit(solution)/shard_map/ppermute | solution.py:175
  74.2 41.6 %all-to-all-done = bf16[64,16,2048]{2,1,0:T(8,128)(2,1)} async-done(((bf16[64,16,2048]{2,1,0:T(8,128)(2,1)}), bf16[64,16,2048]{2,1,0:T(8,128)(2,1)}, u32[]{:S(2)}, u32[]{:S(2)}) %all-to-all-start) | async-done | bytes 4194336 | tf_op jit(solution)/shard_map/all_to_all | solution.py:21
  115.8 5.3 %fusion.24 = bf16[1024,1024]{1,0:T(8,128)(2,1)} fusion(bf16[1024,1024]{1,0:T(8,128)(2,1)S(1)} %select_convert_fusion.weights, bf16[1024,2048]{1,0:T(8,128)(2,1)} %bitcast.5), kind=kOutput, calls=%fused_computation.36 | convolution fusion | flops 2148532224 | bytes 6291456 | tf_op jit(solution)/shard_map/dot_general | solution.py:15
  121.1 5.9 %all-to-all-start.3 = ((bf16[64,16,1024]{2,1,0:T(8,128)(2,1)}), bf16[64,16,1024]{2,1,0:T(8,128)(2,1)}, u32[]{:S(2)}, u32[]{:S(2)}) async-start(bf16[64,16,1024]{2,1,0:T(8,128)(2,1)} %bitcast.59), calls=%async_computation.3 | async-start | bytes 4194304 | tf_op jit(solution)/shard_map/all_to_all | solution.py:21
  127.0 5.2 %fusion.21 = bf16[1024,1024]{1,0:T(8,128)(2,1)} fusion(bf16[1024,1024]{1,0:T(8,128)(2,1)S(1)} %select_convert_fusion.weights, bf16[1024,2048]{1,0:T(8,128)(2,1)} %bitcast.5), kind=kOutput, calls=%fused_computation.35 | convolution fusion | flops 2148532224 | bytes 6291456 | tf_op jit(solution)/shard_map/dot_general | solution.py:15
  132.3 45.9 %all-to-all-done.3 = bf16[64,16,1024]{2,1,0:T(8,128)(2,1)} async-done(((bf16[64,16,1024]{2,1,0:T(8,128)(2,1)}), bf16[64,16,1024]{2,1,0:T(8,128)(2,1)}, u32[]{:S(2)}, u32[]{:S(2)}) %all-to-all-start.3) | async-done | bytes 2097184 | tf_op jit(solution)/shard_map/all_to_all | solution.py:21
  178.1 6.2 %all-to-all-start.1 = ((bf16[64,16,1024]{2,1,0:T(8,128)(2,1)}), bf16[64,16,1024]{2,1,0:T(8,128)(2,1)}, u32[]{:S(2)}, u32[]{:S(2)}) async-start(bf16[64,16,1024]{2,1,0:T(8,128)(2,1)} %bitcast.58), calls=%async_computation.1 | async-start | bytes 4194304 | tf_op jit(solution)/shard_map/all_to_all | solution.py:21
  195.3 40.2 %all-to-all-done.1 = bf16[64,16,1024]{2,1,0:T(8,128)(2,1)} async-done(((bf16[64,16,1024]{2,1,0:T(8,128)(2,1)}), bf16[64,16,1024]{2,1,0:T(8,128)(2,1)}, u32[]{:S(2)}, u32[]{:S(2)}) %all-to-all-start.1) | async-done | bytes 2097184 | tf_op jit(solution)/shard_map/all_to_all | solution.py:21
  249.3 5.8 %all-to-all-start.4 = ((bf16[64,16,1024]{2,1,0:T(8,128)(2,1)}), bf16[64,16,1024]{2,1,0:T(8,128)(2,1)S(1)}, u32[]{:S(2)}, u32[]{:S(2)}) async-start(bf16[64,16,1024]{2,1,0:T(8,128)(2,1)} %bitcast.53), calls=%async_computation.4 | async-start | bytes 4194304 | tf_op jit(solution)/shard_map/all_to_all | solution.py:21
  262.1 19.5 %collective-permute-done.4.moved = bf16[1024,512]{1,0:T(8,128)(2,1)} collective-permute-done((bf16[1024,512]{1,0:T(8,128)(2,1)}, bf16[1024,512]{1,0:T(8,128)(2,1)}, u32[]{:S(2)}, u32[]{:S(2)}) %collective-permute-start.4) | collective-permute-done | bytes 1048608 | tf_op jit(solution)/shard_map/ppermute | solution.py:185
  285.3 18.8 %collective-permute-done.3.moved = bf16[1024,512]{1,0:T(8,128)(2,1)} collective-permute-done((bf16[1024,512]{1,0:T(8,128)(2,1)}, bf16[1024,512]{1,0:T(8,128)(2,1)}, u32[]{:S(2)}, u32[]{:S(2)}) %collective-permute-start.3) | collective-permute-done | bytes 1048608 | tf_op jit(solution)/shard_map/ppermute | solution.py:185
  307.8 11.4 %all-to-all-start.2 = ((bf16[64,16,1024]{2,1,0:T(8,128)(2,1)}), bf16[64,16,1024]{2,1,0:T(8,128)(2,1)}, u32[]{:S(2)}, u32[]{:S(2)}) async-start(bf16[64,16,1024]{2,1,0:T(8,128)(2,1)} %bitcast.52), calls=%async_computation.2 | async-start | bytes 4194304 | tf_op jit(solution)/shard_map/all_to_all | solution.py:21
  319.3 5.4 %shard_map.85.rest_0_ = bf16[1024,2048]{1,0:T(8,128)(2,1)} custom-call(bf16[1024,1024]{1,0:T(8,128)(2,1)} %copy-done.5, bf16[1024,1024]{1,0:T(8,128)(2,1)} %bitcast.57), custom_call_target="tpu_custom_call" | custom-call | flops 2147483648 | bytes 6291456 | tf_op jit(solution)/shard_map/pallas_call | solution.py:111
  324.7 45.7 %all-to-all-done.2 = bf16[64,16,1024]{2,1,0:T(8,128)(2,1)} async-done(((bf16[64,16,1024]{2,1,0:T(8,128)(2,1)}), bf16[64,16,1024]{2,1,0:T(8,128)(2,1)}, u32[]{:S(2)}, u32[]{:S(2)}) %all-to-all-start.2) | async-done | bytes 2097184 | tf_op jit(solution)/shard_map/all_to_all | solution.py:21
  370.4 5.4 %shard_map.86 = bf16[1024,2048]{1,0:T(8,128)(2,1)} custom-call(bf16[1024,1024]{1,0:T(8,128)(2,1)} %copy-done.5, bf16[1024,1024]{1,0:T(8,128)(2,1)} %bitcast.15.columns, bf16[1024,2048]{1,0:T(8,128)(2,1)} %shard_map.85.rest_0_), custom_call_target="tpu_custom_call", output_to_operand_aliasing={{}: (2, {})} | custom-call | flops 2147483648 | bytes 6291456 | tf_op jit(solution)/shard_map/pallas_call | solution.py:111
  375.8 6.2 %all-to-all-start.5 = ((bf16[64,16,2048]{2,1,0:T(8,128)(2,1)}), bf16[64,16,2048]{2,1,0:T(8,128)(2,1)}, u32[]{:S(2)}, u32[]{:S(2)}) async-start(bf16[64,16,2048]{2,1,0:T(8,128)(2,1)} %bitcast.51), calls=%async_computation.5 | async-start | bytes 8388608 | tf_op jit(solution)/shard_map/all_to_all | solution.py:21
  392.7 6.6 %fusion.12 = bf16[1024,2048]{1,0:T(8,128)(2,1)} fusion(bf16[1024,512]{1,0:T(8,128)(2,1)S(1)} %broadcast_select_fusion, bf16[1024,512]{1,0:T(8,128)(2,1)S(1)} %broadcast_select_fusion.1, bf16[1024,512]{1,0:T(8,128)(2,1)S(1)} %broadcast_select_fusion.2, bf16[1024,512]{1,0:T(8,128)(2,1)S(1)} %broadcast_select_fusion.3, s32[1024]{0:T(1024)S(1)} %get-tuple-element.34, ...), kind=kOutput, calls=%fused_computation.24 | convolution fusion | flops 4333764608 | bytes 8416256 | tf_op jit(solution)/shard_map/dot_general | solution.py:15
  399.3 8.2 %collective-permute-done.9 = bf16[1024,512]{1,0:T(8,128)(2,1)S(1)} collective-permute-done((bf16[1024,512]{1,0:T(8,128)(2,1)}, bf16[1024,512]{1,0:T(8,128)(2,1)S(1)}, u32[]{:S(2)}, u32[]{:S(2)}) %collective-permute-start.9) | collective-permute-done | bytes 1048608 | tf_op jit(solution)/shard_map/ppermute | solution.py:209
  408.9 21.1 %collective-permute-done.8 = bf16[1024,512]{1,0:T(8,128)(2,1)S(1)} collective-permute-done((bf16[1024,512]{1,0:T(8,128)(2,1)}, bf16[1024,512]{1,0:T(8,128)(2,1)S(1)}, u32[]{:S(2)}, u32[]{:S(2)}) %collective-permute-start.8) | collective-permute-done | bytes 1048608 | tf_op jit(solution)/shard_map/ppermute | solution.py:209
  433.5 44.3 %all-to-all-done.5 = bf16[64,16,2048]{2,1,0:T(8,128)(2,1)} async-done(((bf16[64,16,2048]{2,1,0:T(8,128)(2,1)}), bf16[64,16,2048]{2,1,0:T(8,128)(2,1)}, u32[]{:S(2)}, u32[]{:S(2)}) %all-to-all-start.5) | async-done | bytes 4194336 | tf_op jit(solution)/shard_map/all_to_all | solution.py:21
  477.8 8.9 %fusion.15 = bf16[1,1024,2048]{2,1,0:T(8,128)(2,1)} fusion(bf16[1024,1024]{1,0:T(8,128)(2,1)S(1)} %copy-done.3, bf16[1024,2048]{1,0:T(8,128)(2,1)} %bitcast.23, f32[2048]{0:T(1024)S(1)} %bitcast.60, bf16[1024,2048]{1,0:T(8,128)(2,1)} %fusion.12), kind=kOutput, calls=%fused_computation.25 | convolution fusion | flops 4303355904 | bytes 14688256 | tf_op jit(solution)/shard_map/dot_general | solution.py:15
  (75 shorter events, 75.7 us)
Async XLA Ops:
  0.6 30.0 %copy-start = (bf16[1,4,256,256]{3,2,1,0:T(8,128)(2,1)S(1)}, bf16[1,4,256,256]{3,2,1,0:T(8,128)(2,1)}, u32[]{:S(2)}) copy-start(bf16[1,4,256,256]{3,2,1,0:T(8,128)(2,1)} %param.8) | copy-start | bytes 1572868
  6.6 109.2 %all-to-all-start = ((bf16[64,16,2048]{2,1,0:T(8,128)(2,1)}), bf16[64,16,2048]{2,1,0:T(8,128)(2,1)}, u32[]{:S(2)}, u32[]{:S(2)}) async-start(bf16[64,16,2048]{2,1,0:T(8,128)(2,1)} %bitcast.56), calls=%async_computation | async-start | bytes 8388608 | tf_op jit(solution)/shard_map/all_to_all | solution.py:21
  22.6 21.8 %collective-permute-start.2 = (bf16[1024,512]{1,0:T(8,128)(2,1)}, bf16[1024,512]{1,0:T(8,128)(2,1)}, u32[]{:S(2)}, u32[]{:S(2)}) collective-permute-start(bf16[1024,512]{1,0:T(8,128)(2,1)} %shard_map.78.here), channel_id=1, source_target_pairs={{128,192},{129,193},{130,194},{131,195},{132,196},{133,197},{134,1... | collective-permute-start | bytes 3145736 | tf_op jit(solution)/shard_map/ppermute | solution.py:175
  24.2 20.1 %collective-permute-start.1 = (bf16[1024,512]{1,0:T(8,128)(2,1)}, bf16[1024,512]{1,0:T(8,128)(2,1)}, u32[]{:S(2)}, u32[]{:S(2)}) collective-permute-start(bf16[1024,512]{1,0:T(8,128)(2,1)} %shard_map.78.here), channel_id=1, source_target_pairs={{64,192},{65,193},{66,194},{67,195},{68,196},{69,197},{70,198},{71... | collective-permute-start | bytes 3145736 | tf_op jit(solution)/shard_map/ppermute | solution.py:175
  25.9 48.3 %collective-permute-start = (bf16[1024,512]{1,0:T(8,128)(2,1)}, bf16[1024,512]{1,0:T(8,128)(2,1)}, u32[]{:S(2)}, u32[]{:S(2)}) collective-permute-start(bf16[1024,512]{1,0:T(8,128)(2,1)} %shard_map.78.here), channel_id=1, source_target_pairs={{0,192},{1,193},{2,194},{3,195},{4,196},{5,197},{6,198},{7,199},{8... | collective-permute-start | bytes 3145736 | tf_op jit(solution)/shard_map/ppermute | solution.py:175
  44.3 82.7 %copy-start.5 = (bf16[1024,1024]{1,0:T(8,128)(2,1)}, bf16[1024,1024]{1,0:T(8,128)(2,1)S(1)}, u32[]{:S(2)}) copy-start(bf16[1024,1024]{1,0:T(8,128)(2,1)S(1)} %select_convert_fusion.weights) | copy-start | bytes 6291460
  121.1 57.1 %all-to-all-start.3 = ((bf16[64,16,1024]{2,1,0:T(8,128)(2,1)}), bf16[64,16,1024]{2,1,0:T(8,128)(2,1)}, u32[]{:S(2)}, u32[]{:S(2)}) async-start(bf16[64,16,1024]{2,1,0:T(8,128)(2,1)} %bitcast.59), calls=%async_computation.3 | async-start | bytes 4194304 | tf_op jit(solution)/shard_map/all_to_all | solution.py:21
  132.3 52.1 %copy-start.12 = (bf16[1,2048]{1,0:T(2,128)(2,1)S(1)}, bf16[1,2048]{1,0:T(2,128)(2,1)}, u32[]{:S(2)}) copy-start(bf16[1,2048]{1,0:T(2,128)(2,1)} %param.11) | copy-start | bytes 12292
  132.3 52.1 %copy-start.9 = (bf16[1024,1024]{1,0:T(8,128)(2,1)S(1)}, bf16[1024,1024]{1,0:T(8,128)(2,1)}, u32[]{:S(2)}) copy-start(bf16[1024,1024]{1,0:T(8,128)(2,1)} %shard_map.79) | copy-start | bytes 6291460
  178.1 57.3 %all-to-all-start.1 = ((bf16[64,16,1024]{2,1,0:T(8,128)(2,1)}), bf16[64,16,1024]{2,1,0:T(8,128)(2,1)}, u32[]{:S(2)}, u32[]{:S(2)}) async-start(bf16[64,16,1024]{2,1,0:T(8,128)(2,1)} %bitcast.58), calls=%async_computation.1 | async-start | bytes 4194304 | tf_op jit(solution)/shard_map/all_to_all | solution.py:21
  188.3 51.6 %collective-permute-start.6 = (bf16[1024,512]{1,0:T(8,128)(2,1)}, bf16[1024,512]{1,0:T(8,128)(2,1)S(1)}, u32[]{:S(2)}, u32[]{:S(2)}) collective-permute-start(bf16[1024,512]{1,0:T(8,128)(2,1)} %add_convert_fusion.1), channel_id=1, source_target_pairs={{64,0},{128,64},{192,128},{65,1},{129,65},{193,129},{66,2},{130,66... | collective-permute-start | bytes 3145736 | tf_op jit(solution)/shard_map/ppermute | solution.py:185
  193.4 51.2 %collective-permute-start.5 = (bf16[1024,512]{1,0:T(8,128)(2,1)}, bf16[1024,512]{1,0:T(8,128)(2,1)S(1)}, u32[]{:S(2)}, u32[]{:S(2)}) collective-permute-start(bf16[1024,512]{1,0:T(8,128)(2,1)} %add_convert_fusion.2), channel_id=1, source_target_pairs={{64,0},{128,64},{192,128},{65,1},{129,65},{193,129},{66,2},{130,66... | collective-permute-start | bytes 3145736 | tf_op jit(solution)/shard_map/ppermute | solution.py:185
  249.3 58.5 %all-to-all-start.4 = ((bf16[64,16,1024]{2,1,0:T(8,128)(2,1)}), bf16[64,16,1024]{2,1,0:T(8,128)(2,1)S(1)}, u32[]{:S(2)}, u32[]{:S(2)}) async-start(bf16[64,16,1024]{2,1,0:T(8,128)(2,1)} %bitcast.53), calls=%async_computation.4 | async-start | bytes 4194304 | tf_op jit(solution)/shard_map/all_to_all | solution.py:21
  255.1 26.5 %collective-permute-start.4 = (bf16[1024,512]{1,0:T(8,128)(2,1)}, bf16[1024,512]{1,0:T(8,128)(2,1)}, u32[]{:S(2)}, u32[]{:S(2)}) collective-permute-start(bf16[1024,512]{1,0:T(8,128)(2,1)} %add_convert_fusion.3), channel_id=1, source_target_pairs={{64,0},{128,64},{192,128},{65,1},{129,65},{193,129},{66,2},{130,66... | collective-permute-start | bytes 3145736 | tf_op jit(solution)/shard_map/ppermute | solution.py:185
  260.8 43.2 %collective-permute-start.3 = (bf16[1024,512]{1,0:T(8,128)(2,1)}, bf16[1024,512]{1,0:T(8,128)(2,1)}, u32[]{:S(2)}, u32[]{:S(2)}) collective-permute-start(bf16[1024,512]{1,0:T(8,128)(2,1)} %add_convert_fusion.4), channel_id=1, source_target_pairs={{64,0},{128,64},{192,128},{65,1},{129,65},{193,129},{66,2},{130,66... | collective-permute-start | bytes 3145736 | tf_op jit(solution)/shard_map/ppermute | solution.py:185
  307.8 11.5 %copy-start.4 = (bf16[64,16,1024]{2,1,0:T(8,128)(2,1)}, bf16[64,16,1024]{2,1,0:T(8,128)(2,1)S(1)}, u32[]{:S(2)}) copy-start(bf16[64,16,1024]{2,1,0:T(8,128)(2,1)S(1)} %all-to-all-done.4) | copy-start | bytes 6291460
  307.8 62.6 %all-to-all-start.2 = ((bf16[64,16,1024]{2,1,0:T(8,128)(2,1)}), bf16[64,16,1024]{2,1,0:T(8,128)(2,1)}, u32[]{:S(2)}, u32[]{:S(2)}) async-start(bf16[64,16,1024]{2,1,0:T(8,128)(2,1)} %bitcast.52), calls=%async_computation.2 | async-start | bytes 4194304 | tf_op jit(solution)/shard_map/all_to_all | solution.py:21
  375.8 14.1 %copy-start.7 = (bf16[1024,512]{1,0:T(8,128)(2,1)S(1)}, bf16[1024,512]{1,0:T(8,128)(2,1)}, u32[]{:S(2)}) copy-start(bf16[1024,512]{1,0:T(8,128)(2,1)} %copy-done.6) | copy-start | bytes 3145732
  375.8 102.0 %all-to-all-start.5 = ((bf16[64,16,2048]{2,1,0:T(8,128)(2,1)}), bf16[64,16,2048]{2,1,0:T(8,128)(2,1)}, u32[]{:S(2)}, u32[]{:S(2)}) async-start(bf16[64,16,2048]{2,1,0:T(8,128)(2,1)} %bitcast.51), calls=%async_computation.5 | async-start | bytes 8388608 | tf_op jit(solution)/shard_map/all_to_all | solution.py:21
  382.0 25.5 %collective-permute-start.9 = (bf16[1024,512]{1,0:T(8,128)(2,1)}, bf16[1024,512]{1,0:T(8,128)(2,1)S(1)}, u32[]{:S(2)}, u32[]{:S(2)}) collective-permute-start(bf16[1024,512]{1,0:T(8,128)(2,1)} %add_convert_fusion.2), channel_id=1, source_target_pairs={{0,64},{1,65},{2,66},{3,67},{4,68},{5,69},{6,70},{7,71},{8,72},{9,... | collective-permute-start | bytes 3145736 | tf_op jit(solution)/shard_map/ppermute | solution.py:209
  385.3 23.6 %collective-permute-start.7 = (bf16[1024,512]{1,0:T(8,128)(2,1)}, bf16[1024,512]{1,0:T(8,128)(2,1)S(1)}, u32[]{:S(2)}, u32[]{:S(2)}) collective-permute-start(bf16[1024,512]{1,0:T(8,128)(2,1)} %add_convert_fusion.4), channel_id=1, source_target_pairs={{0,192},{1,193},{2,194},{3,195},{4,196},{5,197},{6,198},{7,199},{8... | collective-permute-start | bytes 3145736 | tf_op jit(solution)/shard_map/ppermute | solution.py:209
  386.6 43.3 %collective-permute-start.8 = (bf16[1024,512]{1,0:T(8,128)(2,1)}, bf16[1024,512]{1,0:T(8,128)(2,1)S(1)}, u32[]{:S(2)}, u32[]{:S(2)}) collective-permute-start(bf16[1024,512]{1,0:T(8,128)(2,1)} %add_convert_fusion.3), channel_id=1, source_target_pairs={{0,128},{1,129},{2,130},{3,131},{4,132},{5,133},{6,134},{7,135},{8... | collective-permute-start | bytes 3145736 | tf_op jit(solution)/shard_map/ppermute | solution.py:209
  399.3 78.5 %copy-start.3 = (bf16[1024,1024]{1,0:T(8,128)(2,1)S(1)}, bf16[1024,1024]{1,0:T(8,128)(2,1)}, u32[]{:S(2)}) copy-start(bf16[1024,1024]{1,0:T(8,128)(2,1)} %fusion.10.rows_in) | copy-start | bytes 6291460
  477.8 8.9 %copy-start.1 = (bf16[1,4,256,256]{3,2,1,0:T(8,128)(2,1)S(1)}, bf16[1,4,256,256]{3,2,1,0:T(8,128)(2,1)}, u32[]{:S(2)}) copy-start(bf16[1,4,256,256]{3,2,1,0:T(8,128)(2,1)} %param.8) | copy-start | bytes 1572868
  (6 other events, 25.0 us)
where the time goes:
time: 488 us; the launch traced here: 487 us
  waiting for transfers between devices  316 us (65%)
  starting transfers between devices  68.5 us (14%)
  matrix products  49 us (10%)
  Pallas kernels  40.9 us (8%)
  other arithmetic  8.13 us (2%)
    all_to_all x6, waiting for transfers between devices, exchange(): blocks = lax.all_to_all(blocks, 'seq', split_axis=0, concat_axis=0)  218 us
    all_to_all x6, starting transfers between devices, exchange(): blocks = lax.all_to_all(blocks, 'seq', split_axis=0, concat_axis=0)  48.9 us
    dot_general x10, matrix products, dot(): lax.dot_general(a, b, (((1,), (0,)), ((), ())), preferred_element_type=F32)  48.2 us
    ppermute x4, waiting for transfers between devices, step(): return (result, lax.ppermute(result, 'pipe', back))  38.2 us
    ppermute x3, waiting for transfers between devices, local_program(): lax.ppermute(passed[q], 'pipe', [(0, q)])  30.7 us
    ppermute x3, waiting for transfers between devices, local_program(): lax.ppermute(loss_sent, 'pipe', [(q, last)])  29.9 us
    pallas_call x4, Pallas kernels, reorder(): pl.pallas_call(kernel, out_shape=jax.ShapeDtypeStruct(rows_in.shape, BF16...  15.3 us
    pallas_call x4, Pallas kernels, scale_into(): pl.pallas_call(scale_kernel, out_shape=jax.ShapeDtypeStruct((rows, total)...  14.7 us
  transfers between devices with their start and end apart: 16, of which 11 were waited for; matrix products, arithmetic and copies ran while one was open for 9% of the time, Pallas kernels for 6%

commit v1 on v0

--- a/solution.py
+++ b/solution.py
@@ -32,7 +32,7 @@
         starts = [il * order + group * chunk for il in range(count)]
         taken = jnp.concatenate([rows_in[s:s + chunk, :] for s in starts], axis=0)
         if gain is not None:
-            taken = (taken.astype(F32) * gain[...]).astype(BF16)
+            taken = (taken.astype(F32) * gain[...].astype(F32)).astype(BF16)
         rows_out[group * order:(group + 1) * order, :] = dot(place, taken).astype(BF16)
 
 
@@ -60,12 +60,12 @@
 
 def scale_kernel(flag, gain, here, moved, *rest):
     gradient = jnp.where(flag[0] == 1, here[...].astype(F32), moved[...].astype(F32))
-    rest[-1][...] = (gradient * gain[...]).astype(BF16)
+    rest[-1][...] = (gradient * gain[...].astype(F32)).astype(BF16)
 
 
 def scale_into(flag, gain, here, moved, total, at, buffer=None):
     rows, width = here.shape
-    step, column = rows // 4, at // width
+    step, column = rows // 2, at // width
     block = pl.BlockSpec((step, width), lambda n: (n, 0))
     in_specs = [
         pl.BlockSpec(memory_space=pltpu.SMEM),
@@ -82,7 +82,7 @@
     return pl.pallas_call(
         scale_kernel,
         out_shape=jax.ShapeDtypeStruct((rows, total), BF16),
-        grid=(4,),
+        grid=(2,),
         in_specs=in_specs,
         out_specs=pl.BlockSpec((step, width), lambda n: (n, column)),
         input_output_aliases=aliases,
@@ -152,7 +152,7 @@
     wide = jnp.einsum("ikj,kr->ijr", first, pick, preferred_element_type=F32).reshape(rows, rows)
     first_spread = jnp.where(out // order == into // count % count, wide, 0.0).astype(BF16)
 
-    inner, outer = inner_gain.astype(F32), outer_gain.astype(F32)
+    inner, outer = inner_gain, outer_gain.astype(F32)
     restore = (natural.T == into.T).astype(BF16)
     first_sent = reorder(first_spread, count)
 
@@ -195,7 +195,6 @@
     for q in range(per_half):
         buffer = fill(buffer, q)
     passed[per_half], moved[per_half] = step(per_half)
-    buffer, passed[per_half] = lax.optimization_barrier((buffer, passed[per_half]))
     sent.append(exchange(buffer, devices))
     for q in range(per_half + 1, sections):
         passed[q], moved[q] = step(q)

time: 488 us -> 486 us (level)
  starting transfers between devices: 68.5 us -> 74 us
    all_to_all x6, waiting for transfers between devices: 218 us -> 171 us  [exchange(): blocks = lax.all_to_all(blocks, 'seq', split_axis=0, concat_axis=0)]
    ppermute x4, waiting for transfers between devices: 38.2 us -> 78 us  [step(): return (result, lax.ppermute(result, 'pipe', back))]
    ppermute x3, waiting for transfers between devices: 30.7 us -> 37.2 us  [local_program(): lax.ppermute(passed[q], 'pipe', [(0, q)])]
    all_to_all x6, starting transfers between devices: 48.9 us -> 54.4 us  [exchange(): blocks = lax.all_to_all(blocks, 'seq', split_axis=0, concat_axis=0)]
  transfers between devices with their start and end apart: 16 -> 16, of which waited for: 11 -> 12; matrix products, arithmetic and copies ran while one was open for 9% -> 8% of each run, Pallas kernels for 6% -> 5%
where the time goes in v1:
time: 486 us; the launch traced here: 484 us
  waiting for transfers between devices  316 us (65%)
  starting transfers between devices  74 us (15%)
  matrix products  47.6 us (10%)
  Pallas kernels  36.3 us (7%)
  other arithmetic  6.74 us (1%)
    all_to_all x6, waiting for transfers between devices, exchange(): blocks = lax.all_to_all(blocks, 'seq', split_axis=0, concat_axis=0)  171 us
    ppermute x4, waiting for transfers between devices, step(): return (result, lax.ppermute(result, 'pipe', back))  78 us
    all_to_all x6, starting transfers between devices, exchange(): blocks = lax.all_to_all(blocks, 'seq', split_axis=0, concat_axis=0)  54.4 us
    dot_general x10, matrix products, dot(): lax.dot_general(a, b, (((1,), (0,)), ((), ())), preferred_element_type=F32)  46.8 us
    ppermute x3, waiting for transfers between devices, local_program(): lax.ppermute(passed[q], 'pipe', [(0, q)])  37.2 us
    ppermute x3, waiting for transfers between devices, local_program(): lax.ppermute(loss_sent, 'pipe', [(q, last)])  29.9 us
    pallas_call x4, Pallas kernels, reorder(): pl.pallas_call(kernel, out_shape=jax.ShapeDtypeStruct(rows_in.shape, BF16...  15.4 us
    pallas_call x2, Pallas kernels, product_into(): pl.pallas_call(product_kernel, out_shape=jax.ShapeDtypeStruct((rows, tota...  10.8 us
  transfers between devices with their start and end apart: 16, of which 12 were waited for; matrix products, arithmetic and copies ran while one was open for 8% of the time, Pallas kernels for 5%

profile of v1, /device:TPU:1, one launch (start us, length us, event | category | flops | bytes accessed | tf_op | source)
XLA Modules:
  0.0 484.4 jit_solution(16875646348005990575)
XLA Ops:
  5.3 13.3 %all-to-all-start = ((bf16[64,16,2048]{2,1,0:T(8,128)(2,1)}), bf16[64,16,2048]{2,1,0:T(8,128)(2,1)}, u32[]{:S(2)}, u32[]{:S(2)}) async-start(bf16[64,16,2048]{2,1,0:T(8,128)(2,1)} %bitcast.56), calls=%async_computation | async-start | bytes 8388608 | tf_op jit(solution)/shard_map/all_to_all | solution.py:21
  24.6 4.6 collective-permute-start
  43.0 29.9 %collective-permute-done.here = bf16[1024,512]{1,0:T(8,128)(2,1)} collective-permute-done((bf16[1024,512]{1,0:T(8,128)(2,1)}, bf16[1024,512]{1,0:T(8,128)(2,1)}, u32[]{:S(2)}, u32[]{:S(2)}) %collective-permute-start) | collective-permute-done | bytes 1048608 | tf_op jit(solution)/shard_map/ppermute | solution.py:175
  72.9 41.6 %all-to-all-done = bf16[64,16,2048]{2,1,0:T(8,128)(2,1)} async-done(((bf16[64,16,2048]{2,1,0:T(8,128)(2,1)}), bf16[64,16,2048]{2,1,0:T(8,128)(2,1)}, u32[]{:S(2)}, u32[]{:S(2)}) %all-to-all-start) | async-done | bytes 4194336 | tf_op jit(solution)/shard_map/all_to_all | solution.py:21
  114.5 5.3 %fusion.24 = bf16[1024,1024]{1,0:T(8,128)(2,1)} fusion(bf16[1024,1024]{1,0:T(8,128)(2,1)S(1)} %select_convert_fusion.weights, bf16[1024,2048]{1,0:T(8,128)(2,1)} %bitcast.5), kind=kOutput, calls=%fused_computation.36 | convolution fusion | flops 2148532224 | bytes 6291456 | tf_op jit(solution)/shard_map/dot_general | solution.py:15
  119.7 5.9 %all-to-all-start.3 = ((bf16[64,16,1024]{2,1,0:T(8,128)(2,1)}), bf16[64,16,1024]{2,1,0:T(8,128)(2,1)}, u32[]{:S(2)}, u32[]{:S(2)}) async-start(bf16[64,16,1024]{2,1,0:T(8,128)(2,1)} %bitcast.59), calls=%async_computation.3 | async-start | bytes 4194304 | tf_op jit(solution)/shard_map/all_to_all | solution.py:21
  125.7 5.2 %fusion.21 = bf16[1024,1024]{1,0:T(8,128)(2,1)} fusion(bf16[1024,1024]{1,0:T(8,128)(2,1)S(1)} %select_convert_fusion.weights, bf16[1024,2048]{1,0:T(8,128)(2,1)} %bitcast.5), kind=kOutput, calls=%fused_computation.35 | convolution fusion | flops 2148532224 | bytes 6291456 | tf_op jit(solution)/shard_map/dot_general | solution.py:15
  130.9 45.9 %all-to-all-done.3 = bf16[64,16,1024]{2,1,0:T(8,128)(2,1)} async-done(((bf16[64,16,1024]{2,1,0:T(8,128)(2,1)}), bf16[64,16,1024]{2,1,0:T(8,128)(2,1)}, u32[]{:S(2)}, u32[]{:S(2)}) %all-to-all-start.3) | async-done | bytes 2097184 | tf_op jit(solution)/shard_map/all_to_all | solution.py:21
  176.8 6.2 %all-to-all-start.1 = ((bf16[64,16,1024]{2,1,0:T(8,128)(2,1)}), bf16[64,16,1024]{2,1,0:T(8,128)(2,1)}, u32[]{:S(2)}, u32[]{:S(2)}) async-start(bf16[64,16,1024]{2,1,0:T(8,128)(2,1)} %bitcast.58), calls=%async_computation.1 | async-start | bytes 4194304 | tf_op jit(solution)/shard_map/all_to_all | solution.py:21
  194.0 19.4 %collective-permute-done.6.moved = bf16[1024,512]{1,0:T(8,128)(2,1)S(1)} collective-permute-done((bf16[1024,512]{1,0:T(8,128)(2,1)}, bf16[1024,512]{1,0:T(8,128)(2,1)S(1)}, u32[]{:S(2)}, u32[]{:S(2)}) %collective-permute-start.6) | collective-permute-done | bytes 1048608 | tf_op jit(solution)/shard_map/ppermute | solution.py:185
  216.9 18.8 %collective-permute-done.5.moved = bf16[1024,512]{1,0:T(8,128)(2,1)S(1)} collective-permute-done((bf16[1024,512]{1,0:T(8,128)(2,1)}, bf16[1024,512]{1,0:T(8,128)(2,1)S(1)}, u32[]{:S(2)}, u32[]{:S(2)}) %collective-permute-start.5) | collective-permute-done | bytes 1048608 | tf_op jit(solution)/shard_map/ppermute | solution.py:185
  239.3 11.3 %all-to-all-start.4 = ((bf16[64,16,1024]{2,1,0:T(8,128)(2,1)}), bf16[64,16,1024]{2,1,0:T(8,128)(2,1)S(1)}, u32[]{:S(2)}, u32[]{:S(2)}) async-start(bf16[64,16,1024]{2,1,0:T(8,128)(2,1)} %bitcast.53), calls=%async_computation.4 | async-start | bytes 4194304 | tf_op jit(solution)/shard_map/all_to_all | solution.py:21
  260.6 19.9 %collective-permute-done.4.moved = bf16[1024,512]{1,0:T(8,128)(2,1)} collective-permute-done((bf16[1024,512]{1,0:T(8,128)(2,1)S(1)}, bf16[1024,512]{1,0:T(8,128)(2,1)}, u32[]{:S(2)}, u32[]{:S(2)}) %collective-permute-start.4) | collective-permute-done | bytes 1048608 | tf_op jit(solution)/shard_map/ppermute | solution.py:185
  283.0 19.9 %collective-permute-done.3.moved = bf16[1024,512]{1,0:T(8,128)(2,1)} collective-permute-done((bf16[1024,512]{1,0:T(8,128)(2,1)}, bf16[1024,512]{1,0:T(8,128)(2,1)}, u32[]{:S(2)}, u32[]{:S(2)}) %collective-permute-start.3) | collective-permute-done | bytes 1048608 | tf_op jit(solution)/shard_map/ppermute | solution.py:185
  305.5 11.5 %all-to-all-start.2 = ((bf16[64,16,1024]{2,1,0:T(8,128)(2,1)}), bf16[64,16,1024]{2,1,0:T(8,128)(2,1)}, u32[]{:S(2)}, u32[]{:S(2)}) async-start(bf16[64,16,1024]{2,1,0:T(8,128)(2,1)} %bitcast.52), calls=%async_computation.2 | async-start | bytes 4194304 | tf_op jit(solution)/shard_map/all_to_all | solution.py:21
  316.9 5.4 %shard_map.85.rest_0_ = bf16[1024,2048]{1,0:T(8,128)(2,1)} custom-call(bf16[1024,1024]{1,0:T(8,128)(2,1)} %copy-done.5, bf16[1024,1024]{1,0:T(8,128)(2,1)} %bitcast.57), custom_call_target="tpu_custom_call" | custom-call | flops 2147483648 | bytes 6291456 | tf_op jit(solution)/shard_map/pallas_call | solution.py:111
  322.4 45.7 %all-to-all-done.2 = bf16[64,16,1024]{2,1,0:T(8,128)(2,1)} async-done(((bf16[64,16,1024]{2,1,0:T(8,128)(2,1)}), bf16[64,16,1024]{2,1,0:T(8,128)(2,1)}, u32[]{:S(2)}, u32[]{:S(2)}) %all-to-all-start.2) | async-done | bytes 2097184 | tf_op jit(solution)/shard_map/all_to_all | solution.py:21
  368.1 5.4 %shard_map.86 = bf16[1024,2048]{1,0:T(8,128)(2,1)} custom-call(bf16[1024,1024]{1,0:T(8,128)(2,1)} %copy-done.5, bf16[1024,1024]{1,0:T(8,128)(2,1)} %bitcast.15.columns, bf16[1024,2048]{1,0:T(8,128)(2,1)} %shard_map.85.rest_0_), custom_call_target="tpu_custom_call", output_to_operand_aliasing={{}: (2, {})} | custom-call | flops 2147483648 | bytes 6291456 | tf_op jit(solution)/shard_map/pallas_call | solution.py:111
  373.5 6.2 %all-to-all-start.5 = ((bf16[64,16,2048]{2,1,0:T(8,128)(2,1)}), bf16[64,16,2048]{2,1,0:T(8,128)(2,1)}, u32[]{:S(2)}, u32[]{:S(2)}) async-start(bf16[64,16,2048]{2,1,0:T(8,128)(2,1)} %bitcast.51), calls=%async_computation.5 | async-start | bytes 8388608 | tf_op jit(solution)/shard_map/all_to_all | solution.py:21
  390.4 14.8 %collective-permute-done.9 = bf16[1024,512]{1,0:T(8,128)(2,1)S(1)} collective-permute-done((bf16[1024,512]{1,0:T(8,128)(2,1)}, bf16[1024,512]{1,0:T(8,128)(2,1)S(1)}, u32[]{:S(2)}, u32[]{:S(2)}) %collective-permute-start.9) | collective-permute-done | bytes 1048608 | tf_op jit(solution)/shard_map/ppermute | solution.py:208
  406.6 21.1 %collective-permute-done.8 = bf16[1024,512]{1,0:T(8,128)(2,1)S(1)} collective-permute-done((bf16[1024,512]{1,0:T(8,128)(2,1)}, bf16[1024,512]{1,0:T(8,128)(2,1)S(1)}, u32[]{:S(2)}, u32[]{:S(2)}) %collective-permute-start.8) | collective-permute-done | bytes 1048608 | tf_op jit(solution)/shard_map/ppermute | solution.py:208
  431.2 6.5 %fusion.12 = bf16[1024,2048]{1,0:T(8,128)(2,1)} fusion(bf16[1024,512]{1,0:T(8,128)(2,1)S(1)} %broadcast_select_fusion, bf16[1024,512]{1,0:T(8,128)(2,1)S(1)} %broadcast_select_fusion.1, bf16[1024,512]{1,0:T(8,128)(2,1)S(1)} %broadcast_select_fusion.2, bf16[1024,512]{1,0:T(8,128)(2,1)S(1)} %broadcast_select_fusion.3, s32[1024]{0:T(1024)S(1)} %get-tuple-element.30, ...), kind=kOutput, calls=%fused_computation.24 | convolution fusion | flops 4333764608 | bytes 8416256 | tf_op jit(solution)/shard_map/dot_general | solution.py:15
  437.7 37.8 %all-to-all-done.5 = bf16[64,16,2048]{2,1,0:T(8,128)(2,1)} async-done(((bf16[64,16,2048]{2,1,0:T(8,128)(2,1)}), bf16[64,16,2048]{2,1,0:T(8,128)(2,1)}, u32[]{:S(2)}, u32[]{:S(2)}) %all-to-all-start.5) | async-done | bytes 4194336 | tf_op jit(solution)/shard_map/all_to_all | solution.py:21
  475.5 8.9 %fusion.15 = bf16[1,1024,2048]{2,1,0:T(8,128)(2,1)} fusion(bf16[1024,1024]{1,0:T(8,128)(2,1)S(1)} %copy-done.3, bf16[1024,2048]{1,0:T(8,128)(2,1)} %bitcast.23, f32[2048]{0:T(1024)S(1)} %bitcast.60, bf16[1024,2048]{1,0:T(8,128)(2,1)} %fusion.12), kind=kOutput, calls=%fused_computation.25 | convolution fusion | flops 4303355904 | bytes 14688256 | tf_op jit(solution)/shard_map/dot_general | solution.py:15
  (78 shorter events, 72.8 us)
Async XLA Ops:
  0.6 28.7 %copy-start = (bf16[1,4,256,256]{3,2,1,0:T(8,128)(2,1)S(1)}, bf16[1,4,256,256]{3,2,1,0:T(8,128)(2,1)}, u32[]{:S(2)}) copy-start(bf16[1,4,256,256]{3,2,1,0:T(8,128)(2,1)} %param.8) | copy-start | bytes 1572868
  5.3 109.2 %all-to-all-start = ((bf16[64,16,2048]{2,1,0:T(8,128)(2,1)}), bf16[64,16,2048]{2,1,0:T(8,128)(2,1)}, u32[]{:S(2)}, u32[]{:S(2)}) async-start(bf16[64,16,2048]{2,1,0:T(8,128)(2,1)} %bitcast.56), calls=%async_computation | async-start | bytes 8388608 | tf_op jit(solution)/shard_map/all_to_all | solution.py:21
  21.2 21.7 %collective-permute-start.2 = (bf16[1024,512]{1,0:T(8,128)(2,1)}, bf16[1024,512]{1,0:T(8,128)(2,1)}, u32[]{:S(2)}, u32[]{:S(2)}) collective-permute-start(bf16[1024,512]{1,0:T(8,128)(2,1)} %shard_map.78.here), channel_id=1, source_target_pairs={{128,192},{129,193},{130,194},{131,195},{132,196},{133,197},{134,1... | collective-permute-start | bytes 3145736 | tf_op jit(solution)/shard_map/ppermute | solution.py:175
  22.9 20.1 %collective-permute-start.1 = (bf16[1024,512]{1,0:T(8,128)(2,1)}, bf16[1024,512]{1,0:T(8,128)(2,1)}, u32[]{:S(2)}, u32[]{:S(2)}) collective-permute-start(bf16[1024,512]{1,0:T(8,128)(2,1)} %shard_map.78.here), channel_id=1, source_target_pairs={{64,192},{65,193},{66,194},{67,195},{68,196},{69,197},{70,198},{71... | collective-permute-start | bytes 3145736 | tf_op jit(solution)/shard_map/ppermute | solution.py:175
  24.6 48.3 %collective-permute-start = (bf16[1024,512]{1,0:T(8,128)(2,1)}, bf16[1024,512]{1,0:T(8,128)(2,1)}, u32[]{:S(2)}, u32[]{:S(2)}) collective-permute-start(bf16[1024,512]{1,0:T(8,128)(2,1)} %shard_map.78.here), channel_id=1, source_target_pairs={{0,192},{1,193},{2,194},{3,195},{4,196},{5,197},{6,198},{7,199},{8... | collective-permute-start | bytes 3145736 | tf_op jit(solution)/shard_map/ppermute | solution.py:175
  42.9 82.8 %copy-start.5 = (bf16[1024,1024]{1,0:T(8,128)(2,1)}, bf16[1024,1024]{1,0:T(8,128)(2,1)S(1)}, u32[]{:S(2)}) copy-start(bf16[1024,1024]{1,0:T(8,128)(2,1)S(1)} %select_convert_fusion.weights) | copy-start | bytes 6291460
  119.7 57.1 %all-to-all-start.3 = ((bf16[64,16,1024]{2,1,0:T(8,128)(2,1)}), bf16[64,16,1024]{2,1,0:T(8,128)(2,1)}, u32[]{:S(2)}, u32[]{:S(2)}) async-start(bf16[64,16,1024]{2,1,0:T(8,128)(2,1)} %bitcast.59), calls=%async_computation.3 | async-start | bytes 4194304 | tf_op jit(solution)/shard_map/all_to_all | solution.py:21
  130.9 52.1 %copy-start.13 = (bf16[1,2048]{1,0:T(2,128)(2,1)S(1)}, bf16[1,2048]{1,0:T(2,128)(2,1)}, u32[]{:S(2)}) copy-start(bf16[1,2048]{1,0:T(2,128)(2,1)} %param.11) | copy-start | bytes 12292
  130.9 52.1 %copy-start.9 = (bf16[1024,1024]{1,0:T(8,128)(2,1)S(1)}, bf16[1024,1024]{1,0:T(8,128)(2,1)}, u32[]{:S(2)}) copy-start(bf16[1024,1024]{1,0:T(8,128)(2,1)} %shard_map.79) | copy-start | bytes 6291460
  176.8 62.5 %all-to-all-start.1 = ((bf16[64,16,1024]{2,1,0:T(8,128)(2,1)}), bf16[64,16,1024]{2,1,0:T(8,128)(2,1)}, u32[]{:S(2)}, u32[]{:S(2)}) async-start(bf16[64,16,1024]{2,1,0:T(8,128)(2,1)} %bitcast.58), calls=%async_computation.1 | async-start | bytes 4194304 | tf_op jit(solution)/shard_map/all_to_all | solution.py:21
  187.0 26.4 %collective-permute-start.6 = (bf16[1024,512]{1,0:T(8,128)(2,1)}, bf16[1024,512]{1,0:T(8,128)(2,1)S(1)}, u32[]{:S(2)}, u32[]{:S(2)}) collective-permute-start(bf16[1024,512]{1,0:T(8,128)(2,1)} %add_convert_fusion.1), channel_id=1, source_target_pairs={{64,0},{128,64},{192,128},{65,1},{129,65},{193,129},{66,2},{130,66... | collective-permute-start | bytes 3145736 | tf_op jit(solution)/shard_map/ppermute | solution.py:185
  192.1 43.6 %collective-permute-start.5 = (bf16[1024,512]{1,0:T(8,128)(2,1)}, bf16[1024,512]{1,0:T(8,128)(2,1)S(1)}, u32[]{:S(2)}, u32[]{:S(2)}) collective-permute-start(bf16[1024,512]{1,0:T(8,128)(2,1)} %add_convert_fusion.2), channel_id=1, source_target_pairs={{64,0},{128,64},{192,128},{65,1},{129,65},{193,129},{66,2},{130,66... | collective-permute-start | bytes 3145736 | tf_op jit(solution)/shard_map/ppermute | solution.py:185
  239.3 66.2 %all-to-all-start.4 = ((bf16[64,16,1024]{2,1,0:T(8,128)(2,1)}), bf16[64,16,1024]{2,1,0:T(8,128)(2,1)S(1)}, u32[]{:S(2)}, u32[]{:S(2)}) async-start(bf16[64,16,1024]{2,1,0:T(8,128)(2,1)} %bitcast.53), calls=%async_computation.4 | async-start | bytes 4194304 | tf_op jit(solution)/shard_map/all_to_all | solution.py:21
  254.2 26.3 %collective-permute-start.4 = (bf16[1024,512]{1,0:T(8,128)(2,1)S(1)}, bf16[1024,512]{1,0:T(8,128)(2,1)}, u32[]{:S(2)}, u32[]{:S(2)}) collective-permute-start(bf16[1024,512]{1,0:T(8,128)(2,1)S(1)} %add_convert_fusion.3), channel_id=1, source_target_pairs={{64,0},{128,64},{192,128},{65,1},{129,65},{193,129},{66,2},{130,66... | collective-permute-start | bytes 3145736 | tf_op jit(solution)/shard_map/ppermute | solution.py:185
  259.3 43.6 %collective-permute-start.3 = (bf16[1024,512]{1,0:T(8,128)(2,1)}, bf16[1024,512]{1,0:T(8,128)(2,1)}, u32[]{:S(2)}, u32[]{:S(2)}) collective-permute-start(bf16[1024,512]{1,0:T(8,128)(2,1)} %add_convert_fusion.4), channel_id=1, source_target_pairs={{64,0},{128,64},{192,128},{65,1},{129,65},{193,129},{66,2},{130,66... | collective-permute-start | bytes 3145736 | tf_op jit(solution)/shard_map/ppermute | solution.py:185
  305.5 11.5 %copy-start.4 = (bf16[64,16,1024]{2,1,0:T(8,128)(2,1)}, bf16[64,16,1024]{2,1,0:T(8,128)(2,1)S(1)}, u32[]{:S(2)}) copy-start(bf16[64,16,1024]{2,1,0:T(8,128)(2,1)S(1)} %all-to-all-done.4) | copy-start | bytes 6291460
  305.5 62.6 %all-to-all-start.2 = ((bf16[64,16,1024]{2,1,0:T(8,128)(2,1)}), bf16[64,16,1024]{2,1,0:T(8,128)(2,1)}, u32[]{:S(2)}, u32[]{:S(2)}) async-start(bf16[64,16,1024]{2,1,0:T(8,128)(2,1)} %bitcast.52), calls=%async_computation.2 | async-start | bytes 4194304 | tf_op jit(solution)/shard_map/all_to_all | solution.py:21
  373.5 14.1 %copy-start.7 = (bf16[1024,512]{1,0:T(8,128)(2,1)S(1)}, bf16[1024,512]{1,0:T(8,128)(2,1)}, u32[]{:S(2)}) copy-start(bf16[1024,512]{1,0:T(8,128)(2,1)} %copy-done.6) | copy-start | bytes 3145732
  373.5 102.0 %all-to-all-start.5 = ((bf16[64,16,2048]{2,1,0:T(8,128)(2,1)}), bf16[64,16,2048]{2,1,0:T(8,128)(2,1)}, u32[]{:S(2)}, u32[]{:S(2)}) async-start(bf16[64,16,2048]{2,1,0:T(8,128)(2,1)} %bitcast.51), calls=%async_computation.5 | async-start | bytes 8388608 | tf_op jit(solution)/shard_map/all_to_all | solution.py:21
  379.7 25.5 %collective-permute-start.9 = (bf16[1024,512]{1,0:T(8,128)(2,1)}, bf16[1024,512]{1,0:T(8,128)(2,1)S(1)}, u32[]{:S(2)}, u32[]{:S(2)}) collective-permute-start(bf16[1024,512]{1,0:T(8,128)(2,1)} %add_convert_fusion.2), channel_id=1, source_target_pairs={{0,64},{1,65},{2,66},{3,67},{4,68},{5,69},{6,70},{7,71},{8,72},{9,... | collective-permute-start | bytes 3145736 | tf_op jit(solution)/shard_map/ppermute | solution.py:208
  383.0 23.6 %collective-permute-start.7 = (bf16[1024,512]{1,0:T(8,128)(2,1)}, bf16[1024,512]{1,0:T(8,128)(2,1)S(1)}, u32[]{:S(2)}, u32[]{:S(2)}) collective-permute-start(bf16[1024,512]{1,0:T(8,128)(2,1)} %add_convert_fusion.4), channel_id=1, source_target_pairs={{0,192},{1,193},{2,194},{3,195},{4,196},{5,197},{6,198},{7,199},{8... | collective-permute-start | bytes 3145736 | tf_op jit(solution)/shard_map/ppermute | solution.py:208
  384.3 43.3 %collective-permute-start.8 = (bf16[1024,512]{1,0:T(8,128)(2,1)}, bf16[1024,512]{1,0:T(8,128)(2,1)S(1)}, u32[]{:S(2)}, u32[]{:S(2)}) collective-permute-start(bf16[1024,512]{1,0:T(8,128)(2,1)} %copy-done.14), channel_id=1, source_target_pairs={{0,128},{1,129},{2,130},{3,131},{4,132},{5,133},{6,134},{7,135},{8... | collective-permute-start | bytes 3145736 | tf_op jit(solution)/shard_map/ppermute | solution.py:208
  431.2 44.3 %copy-start.3 = (bf16[1024,1024]{1,0:T(8,128)(2,1)S(1)}, bf16[1024,1024]{1,0:T(8,128)(2,1)}, u32[]{:S(2)}) copy-start(bf16[1024,1024]{1,0:T(8,128)(2,1)} %fusion.10.rows_in) | copy-start | bytes 6291460
  475.5 8.9 %copy-start.1 = (bf16[1,4,256,256]{3,2,1,0:T(8,128)(2,1)S(1)}, bf16[1,4,256,256]{3,2,1,0:T(8,128)(2,1)}, u32[]{:S(2)}) copy-start(bf16[1,4,256,256]{3,2,1,0:T(8,128)(2,1)} %param.8) | copy-start | bytes 1572868
  (8 other events, 34.9 us)

commit v2 on v1

--- a/solution.py
+++ b/solution.py
@@ -165,7 +165,6 @@
 
     whole = slice(0, channels)
     halves = (slice(0, channels // 2), slice(channels // 2, channels))
-    pieces = [slice(q * piece, (q + 1) * piece) for q in range(sections)]
     per_half = sections // 2
 
     first_sending = exchange(reorder(arriving[0], count, inner), devices)
@@ -173,45 +172,60 @@
     reordered = reorder(arriving[0], count)
     loss_sent = reorder(loss_grad, count)
     lost = [loss_sent if q == last else lax.ppermute(loss_sent, "pipe", [(q, last)]) for q in range(sections)]
-    columns, lost, first_sent, reordered = lax.optimization_barrier((first_sending, lost, first_sent, reordered))
+    around = piece // sections
+    cuts = ((0, piece - around, False), (piece - around, around, True), (piece, piece, False))
+    here = [
+        [lost[n * per_half + start // piece][:, start % piece:start % piece + width] for start, width, _ in cuts]
+        for n in range(2)
+    ]
+    columns, here, first_sent, reordered = lax.optimization_barrier((first_sending, here, first_sent, reordered))
 
     back = [(i + 1, i) for i in range(sections - 1)]
     returned = [exchange(mix(columns[:, h]), devices) for h in halves]
     flag = (position == last).astype(jnp.int32).reshape(1)
 
-    def step(q):
-        cut = slice(q % per_half * piece, (q % per_half + 1) * piece)
-        result = finish(reordered[:, pieces[q]], first_sent, returned[q // per_half][:, cut], pieces[q])
-        return result, lax.ppermute(result, "pipe", back)
-
-    def fill(buffer, q):
-        at = q % per_half * piece
-        return scale_into(flag, inner[:, pieces[q]], lost[q], moved[q], channels // 2, at, buffer)
-
-    passed, moved, sent = [None] * sections, [None] * sections, []
-    for q in range(per_half):
-        passed[q], moved[q] = step(q)
-    buffer = None
-    for q in range(per_half):
-        buffer = fill(buffer, q)
-    passed[per_half], moved[per_half] = step(per_half)
-    sent.append(exchange(buffer, devices))
-    for q in range(per_half + 1, sections):
-        passed[q], moved[q] = step(q)
-    buffer = None
-    for q in range(per_half, sections):
-        buffer = fill(buffer, q)
-    sent.append(exchange(buffer, devices))
-
-    leaving = passed[0]
+    def shift(block, round_about):
+        if not round_about:
+            return lax.ppermute(block, "pipe", back)
+        for hop in range(last):
+            route = [((i + 1 + hop) % sections, (i + 2 + hop) % sections) for i in range(last)]
+            block = lax.ppermute(block, "pipe", route)
+        return block
+
+    def step(n):
+        passed, moved = [], []
+        for c, (start, width, round_about) in enumerate(cuts):
+            cols = slice(halves[n].start + start, halves[n].start + start + width)
+            passed.append(finish(reordered[:, cols], first_sent, returned[n][:, start:start + width], cols))
+            moved.append(shift(passed[c], round_about))
+        return passed, moved
+
+    def fill(n, moved):
+        buffer = None
+        for c in (1, 2, 0):
+            start, width, _ = cuts[c]
+            gain = inner[:, halves[n].start + start:halves[n].start + start + width]
+            buffer = scale_into(flag, gain, here[n][c], moved[c], channels // 2, start, buffer)
+        return buffer
+
+    passed, moved, sent = [], [], []
+    for n in range(2):
+        done, shifted = step(n)
+        sent.append(exchange(fill(n, shifted), devices))
+        passed.append(done)
+        moved += shifted
+
+    leaving = jnp.concatenate(passed[0][:2], axis=1)
     for q in range(1, sections):
-        leaving = jnp.where(position == q, lax.ppermute(passed[q], "pipe", [(0, q)]), leaving)
+        parts = passed[q // per_half][:2] if q % per_half == 0 else passed[q // per_half][2:]
+        parts = jnp.concatenate([lax.ppermute(p, "pipe", [(0, q)]) for p in parts], axis=1)
+        leaving = jnp.where(position == q, parts, leaving)
     leaving = dot(restore, leaving).astype(BF16)
 
     mixed = product_into(second_spread, sent[0], channels, 0)
     mixed = product_into(second_spread, sent[1], channels, channels // 2, mixed)
     final = exchange(mixed, devices)
-    source = jnp.concatenate([jnp.where(position == last, a, b) for a, b in zip(lost, moved)], axis=1)
+    source = jnp.concatenate([jnp.where(position == last, a, b) for a, b in zip(here[0] + here[1], moved)], axis=1)
     source = dot(restore, source).astype(BF16)
     final, source, leaving = lax.optimization_barrier((final, source, leaving))
     entering = finish(source, first_spread, final, whole)

time: 486 us -> 486 us (level)
  waiting for transfers between devices: 316 us -> 278 us
  starting transfers between devices: 74 us -> 94.4 us
  local copies, waits for them, and re-layouts: 2.67 us -> 13.9 us
    ppermute x7 -> x14, waiting for transfers between devices: 115 us -> 84.5 us  [the longest x4 35.4 us: local_program(): lax.ppermute(p, 'pipe', [(0, q)])]
    ppermute x7 -> x14, starting transfers between devices: 11.7 us -> 32 us  [the longest x6 18.8 us: shift(): block = lax.ppermute(block, 'pipe', route)]
    slice x1 -> x7, local copies, waits for them, and re-layouts: 0.61 us -> 9.48 us  [the longest x4 7.79 us: local_program(): lost[n * per_half + start // piece][:, start % piece:start % piece + width]]
    pallas_call x4 -> x6, Pallas kernels: 10.1 us -> 13.3 us  [scale_into(): pl.pallas_call(scale_kernel, out_shape=jax.ShapeDtypeStruct((rows, total)...]
    dot_general x10 -> x12, matrix products: 46.8 us -> 49 us  [dot(): lax.dot_general(a, b, (((1,), (0,)), ((), ())), preferred_element_type=F32)]
  transfers between devices with their start and end apart: 16 -> 23, of which waited for: 12 -> 13; matrix products, arithmetic and copies ran while one was open for 8% -> 11% of each run, Pallas kernels for 5% -> 6%
where the time goes in v2:
time: 486 us; the launch traced here: 485 us
  waiting for transfers between devices  278 us (57%)
  starting transfers between devices  94.4 us (19%)
  matrix products  49.8 us (10%)
  Pallas kernels  39.4 us (8%)
  local copies, waits for them, and re-layouts  13.9 us (3%)
  other arithmetic  7.45 us (2%)
    all_to_all x6, waiting for transfers between devices, exchange(): blocks = lax.all_to_all(blocks, 'seq', split_axis=0, concat_axis=0)  168 us
    all_to_all x6, starting transfers between devices, exchange(): blocks = lax.all_to_all(blocks, 'seq', split_axis=0, concat_axis=0)  54.4 us
    dot_general x12, matrix products, dot(): lax.dot_general(a, b, (((1,), (0,)), ((), ())), preferred_element_type=F32)  49 us
    ppermute x4, waiting for transfers between devices, local_program(): lax.ppermute(p, 'pipe', [(0, q)])  35.4 us
    ppermute x6, waiting for transfers between devices, shift(): block = lax.ppermute(block, 'pipe', route)  27.7 us
    ppermute x3, waiting for transfers between devices, local_program(): lax.ppermute(loss_sent, 'pipe', [(q, last)])  25.9 us
    ppermute x4, waiting for transfers between devices, shift(): return lax.ppermute(block, 'pipe', back)  21.3 us
    ppermute x6, starting transfers between devices, shift(): block = lax.ppermute(block, 'pipe', route)  18.8 us
  transfers between devices with their start and end apart: 23, of which 13 were waited for; matrix products, arithmetic and copies ran while one was open for 11% of the time, Pallas kernels for 6%

profile of v2, /device:TPU:1, one launch (start us, length us, event | category | flops | bytes accessed | tf_op | source)
XLA Modules:
  0.0 484.6 jit_solution(9960228259129385052)
XLA Ops:
  5.3 13.3 %all-to-all-start = ((bf16[64,16,2048]{2,1,0:T(8,128)(2,1)}), bf16[64,16,2048]{2,1,0:T(8,128)(2,1)}, u32[]{:S(2)}, u32[]{:S(2)}) async-start(bf16[64,16,2048]{2,1,0:T(8,128)(2,1)} %bitcast.61), calls=%async_computation | async-start | bytes 8388608 | tf_op jit(solution)/shard_map/all_to_all | solution.py:21
  47.0 25.9 %collective-permute-done = bf16[1024,512]{1,0:T(8,128)(2,1)} collective-permute-done((bf16[1024,512]{1,0:T(8,128)(2,1)}, bf16[1024,512]{1,0:T(8,128)(2,1)}, u32[]{:S(2)}, u32[]{:S(2)}) %collective-permute-start) | collective-permute-done | bytes 1048608 | tf_op jit(solution)/shard_map/ppermute | solution.py:174
  76.6 37.8 %all-to-all-done = bf16[64,16,2048]{2,1,0:T(8,128)(2,1)} async-done(((bf16[64,16,2048]{2,1,0:T(8,128)(2,1)}), bf16[64,16,2048]{2,1,0:T(8,128)(2,1)}, u32[]{:S(2)}, u32[]{:S(2)}) %all-to-all-start) | async-done | bytes 4194336 | tf_op jit(solution)/shard_map/all_to_all | solution.py:21
  119.7 5.9 %all-to-all-start.3 = ((bf16[64,16,1024]{2,1,0:T(8,128)(2,1)}), bf16[64,16,1024]{2,1,0:T(8,128)(2,1)}, u32[]{:S(2)}, u32[]{:S(2)}) async-start(bf16[64,16,1024]{2,1,0:T(8,128)(2,1)} %bitcast.64), calls=%async_computation.3 | async-start | bytes 4194304 | tf_op jit(solution)/shard_map/all_to_all | solution.py:21
  130.9 45.9 %all-to-all-done.3 = bf16[64,16,1024]{2,1,0:T(8,128)(2,1)} async-done(((bf16[64,16,1024]{2,1,0:T(8,128)(2,1)}), bf16[64,16,1024]{2,1,0:T(8,128)(2,1)}, u32[]{:S(2)}, u32[]{:S(2)}) %all-to-all-start.3) | async-done | bytes 2097184 | tf_op jit(solution)/shard_map/all_to_all | solution.py:21
  176.8 6.2 %all-to-all-start.1 = ((bf16[64,16,1024]{2,1,0:T(8,128)(2,1)}), bf16[64,16,1024]{2,1,0:T(8,128)(2,1)}, u32[]{:S(2)}, u32[]{:S(2)}) async-start(bf16[64,16,1024]{2,1,0:T(8,128)(2,1)} %bitcast.63), calls=%async_computation.1 | async-start | bytes 4194304 | tf_op jit(solution)/shard_map/all_to_all | solution.py:21
  195.4 6.2 %collective-permute-start.11 = (bf16[1024,128]{1,0:T(8,128)(2,1)S(1)}, bf16[1024,128]{1,0:T(8,128)(2,1)S(1)}, u32[]{:S(2)}, u32[]{:S(2)}) collective-permute-start(bf16[1024,128]{1,0:T(8,128)(2,1)S(1)} %collective-permute-done.10), channel_id=1, source_target_pairs={{128,192},{192,0},{0,64},{129,193},{193,1},{1,65},{130,194},{194,2... | collective-permute-start | bytes 786440 | tf_op jit(solution)/shard_map/ppermute | solution.py:192
  202.2 6.9 %collective-permute-done.11 = bf16[1024,128]{1,0:T(8,128)(2,1)S(1)} collective-permute-done((bf16[1024,128]{1,0:T(8,128)(2,1)S(1)}, bf16[1024,128]{1,0:T(8,128)(2,1)S(1)}, u32[]{:S(2)}, u32[]{:S(2)}) %collective-permute-start.11) | collective-permute-done | bytes 262176 | tf_op jit(solution)/shard_map/ppermute | solution.py:192
  212.2 6.2 %collective-permute-done.12.moved = bf16[1024,128]{1,0:T(8,128)(2,1)S(1)} collective-permute-done((bf16[1024,128]{1,0:T(8,128)(2,1)S(1)}, bf16[1024,128]{1,0:T(8,128)(2,1)S(1)}, u32[]{:S(2)}, u32[]{:S(2)}) %collective-permute-start.12) | collective-permute-done | bytes 262176 | tf_op jit(solution)/shard_map/ppermute | solution.py:192
  224.4 10.4 %collective-permute-done.8.moved = bf16[1024,384]{1,0:T(8,128)(2,1)S(1)} collective-permute-done((bf16[1024,384]{1,0:T(8,128)(2,1)S(1)}, bf16[1024,384]{1,0:T(8,128)(2,1)S(1)}, u32[]{:S(2)}, u32[]{:S(2)}) %collective-permute-start.8) | collective-permute-done | bytes 786464 | tf_op jit(solution)/shard_map/ppermute | solution.py:189
  238.1 11.3 %all-to-all-start.4 = ((bf16[64,16,1024]{2,1,0:T(8,128)(2,1)}), bf16[64,16,1024]{2,1,0:T(8,128)(2,1)S(1)}, u32[]{:S(2)}, u32[]{:S(2)}) async-start(bf16[64,16,1024]{2,1,0:T(8,128)(2,1)} %bitcast.58), calls=%async_computation.4 | async-start | bytes 4194304 | tf_op jit(solution)/shard_map/all_to_all | solution.py:21
  263.9 6.1 %collective-permute-start.6 = (bf16[1024,128]{1,0:T(8,128)(2,1)S(1)}, bf16[1024,128]{1,0:T(8,128)(2,1)S(1)}, u32[]{:S(2)}, u32[]{:S(2)}) collective-permute-start(bf16[1024,128]{1,0:T(8,128)(2,1)S(1)} %collective-permute-done.5), channel_id=1, source_target_pairs={{128,192},{192,0},{0,64},{129,193},{193,1},{1,65},{130,194},{194,2... | collective-permute-start | bytes 786440 | tf_op jit(solution)/shard_map/ppermute | solution.py:192
  270.0 7.5 %collective-permute-done.6 = bf16[1024,128]{1,0:T(8,128)(2,1)S(1)} collective-permute-done((bf16[1024,128]{1,0:T(8,128)(2,1)S(1)}, bf16[1024,128]{1,0:T(8,128)(2,1)S(1)}, u32[]{:S(2)}, u32[]{:S(2)}) %collective-permute-start.6) | collective-permute-done | bytes 262176 | tf_op jit(solution)/shard_map/ppermute | solution.py:192
  279.4 7.2 %collective-permute-done.7.moved = bf16[1024,128]{1,0:T(8,128)(2,1)S(1)} collective-permute-done((bf16[1024,128]{1,0:T(8,128)(2,1)S(1)}, bf16[1024,128]{1,0:T(8,128)(2,1)S(1)}, u32[]{:S(2)}, u32[]{:S(2)}) %collective-permute-start.7) | collective-permute-done | bytes 262176 | tf_op jit(solution)/shard_map/ppermute | solution.py:192
  291.6 10.9 %collective-permute-done.3.moved = bf16[1024,384]{1,0:T(8,128)(2,1)S(1)} collective-permute-done((bf16[1024,384]{1,0:T(8,128)(2,1)}, bf16[1024,384]{1,0:T(8,128)(2,1)S(1)}, u32[]{:S(2)}, u32[]{:S(2)}) %collective-permute-start.3) | collective-permute-done | bytes 786464 | tf_op jit(solution)/shard_map/ppermute | solution.py:189
  305.7 11.4 %all-to-all-start.2 = ((bf16[64,16,1024]{2,1,0:T(8,128)(2,1)}), bf16[64,16,1024]{2,1,0:T(8,128)(2,1)}, u32[]{:S(2)}, u32[]{:S(2)}) async-start(bf16[64,16,1024]{2,1,0:T(8,128)(2,1)} %bitcast.57), calls=%async_computation.2 | async-start | bytes 4194304 | tf_op jit(solution)/shard_map/all_to_all | solution.py:21
  317.1 5.4 %shard_map.87.rest_0_ = bf16[1024,2048]{1,0:T(8,128)(2,1)} custom-call(bf16[1024,1024]{1,0:T(8,128)(2,1)} %copy-done.5, bf16[1024,1024]{1,0:T(8,128)(2,1)} %bitcast.62), custom_call_target="tpu_custom_call" | custom-call | flops 2147483648 | bytes 6291456 | tf_op jit(solution)/shard_map/pallas_call | solution.py:111
  322.6 45.7 %all-to-all-done.2 = bf16[64,16,1024]{2,1,0:T(8,128)(2,1)} async-done(((bf16[64,16,1024]{2,1,0:T(8,128)(2,1)}), bf16[64,16,1024]{2,1,0:T(8,128)(2,1)}, u32[]{:S(2)}, u32[]{:S(2)}) %all-to-all-start.2) | async-done | bytes 2097184 | tf_op jit(solution)/shard_map/all_to_all | solution.py:21
  373.7 6.2 %all-to-all-start.5 = ((bf16[64,16,2048]{2,1,0:T(8,128)(2,1)}), bf16[64,16,2048]{2,1,0:T(8,128)(2,1)}, u32[]{:S(2)}, u32[]{:S(2)}) async-start(bf16[64,16,2048]{2,1,0:T(8,128)(2,1)} %bitcast.56), calls=%async_computation.5 | async-start | bytes 8388608 | tf_op jit(solution)/shard_map/all_to_all | solution.py:21
  393.1 12.9 %collective-permute-done.14 = bf16[1024,384]{1,0:T(8,128)(2,1)S(1)} collective-permute-done((bf16[1024,384]{1,0:T(8,128)(2,1)}, bf16[1024,384]{1,0:T(8,128)(2,1)S(1)}, u32[]{:S(2)}, u32[]{:S(2)}) %collective-permute-start.14) | collective-permute-done | bytes 786464 | tf_op jit(solution)/shard_map/ppermute | solution.py:221
  406.0 22.5 %collective-permute-done.16 = bf16[1024,512]{1,0:T(8,128)(2,1)S(1)} collective-permute-done((bf16[1024,512]{1,0:T(8,128)(2,1)}, bf16[1024,512]{1,0:T(8,128)(2,1)S(1)}, u32[]{:S(2)}, u32[]{:S(2)}) %collective-permute-start.16) | collective-permute-done | bytes 1048608 | tf_op jit(solution)/shard_map/ppermute | solution.py:221
  430.9 6.1 %convolution_convert_fusion = bf16[1024,2048]{1,0:T(8,128)(2,1)} fusion(bf16[1024,2048]{1,0:T(8,128)(2,1)S(1)} %select_dynamic-update-slice_fusion, s32[1024]{0:T(1024)S(1)} %get-tuple-element.38, s32[1024]{0:T(1024)S(1)} %get-tuple-element.41, s32[1024]{0:T(1024)S(1)} %get-tuple-element.43, s32[1024]{0:T(1024)S(1)} %broadcast_add_fusion.2, ...), kind=kOutput, calls=%fused_computation.16 | convolution fusion | flops 4316987392 | bytes 8416256 | tf_op jit(solution)/shard_map/dot_general | solution.py:15
  437.0 38.7 %all-to-all-done.5 = bf16[64,16,2048]{2,1,0:T(8,128)(2,1)} async-done(((bf16[64,16,2048]{2,1,0:T(8,128)(2,1)}), bf16[64,16,2048]{2,1,0:T(8,128)(2,1)}, u32[]{:S(2)}, u32[]{:S(2)}) %all-to-all-start.5) | async-done | bytes 4194336 | tf_op jit(solution)/shard_map/all_to_all | solution.py:21
  475.7 8.9 %fusion.4 = bf16[1,1024,2048]{2,1,0:T(8,128)(2,1)} fusion(bf16[1024,1024]{1,0:T(8,128)(2,1)S(1)} %copy-done.3, bf16[1024,2048]{1,0:T(8,128)(2,1)} %bitcast.23, f32[2048]{0:T(1024)S(1)} %bitcast.65, bf16[1024,2048]{1,0:T(8,128)(2,1)} %convolution_convert_fusion), kind=kOutput, calls=%fused_computation.17 | convolution fusion | flops 4303355904 | bytes 14688256 | tf_op jit(solution)/shard_map/dot_general | solution.py:15
  (132 shorter events, 117.7 us)
Async XLA Ops:
  5.3 109.2 %all-to-all-start = ((bf16[64,16,2048]{2,1,0:T(8,128)(2,1)}), bf16[64,16,2048]{2,1,0:T(8,128)(2,1)}, u32[]{:S(2)}, u32[]{:S(2)}) async-start(bf16[64,16,2048]{2,1,0:T(8,128)(2,1)} %bitcast.61), calls=%async_computation | async-start | bytes 8388608 | tf_op jit(solution)/shard_map/all_to_all | solution.py:21
  21.2 21.7 %collective-permute-start.2 = (bf16[1024,512]{1,0:T(8,128)(2,1)}, bf16[1024,512]{1,0:T(8,128)(2,1)}, u32[]{:S(2)}, u32[]{:S(2)}) collective-permute-start(bf16[1024,512]{1,0:T(8,128)(2,1)} %shard_map.78.here), channel_id=1, source_target_pairs={{128,192},{129,193},{130,194},{131,195},{132,196},{133,197},{134,1... | collective-permute-start | bytes 3145736 | tf_op jit(solution)/shard_map/ppermute | solution.py:174
  22.9 53.7 %collective-permute-start.1 = (bf16[1024,512]{1,0:T(8,128)(2,1)}, bf16[1024,512]{1,0:T(8,128)(2,1)}, u32[]{:S(2)}, u32[]{:S(2)}) collective-permute-start(bf16[1024,512]{1,0:T(8,128)(2,1)} %shard_map.78.here), channel_id=1, source_target_pairs={{64,192},{65,193},{66,194},{67,195},{68,196},{69,197},{70,198},{71... | collective-permute-start | bytes 3145736 | tf_op jit(solution)/shard_map/ppermute | solution.py:174
  24.5 48.3 %collective-permute-start = (bf16[1024,512]{1,0:T(8,128)(2,1)}, bf16[1024,512]{1,0:T(8,128)(2,1)}, u32[]{:S(2)}, u32[]{:S(2)}) collective-permute-start(bf16[1024,512]{1,0:T(8,128)(2,1)} %shard_map.78.here), channel_id=1, source_target_pairs={{0,192},{1,193},{2,194},{3,195},{4,196},{5,197},{6,198},{7,199},{8... | collective-permute-start | bytes 3145736 | tf_op jit(solution)/shard_map/ppermute | solution.py:174
  42.9 82.8 %copy-start.5 = (bf16[1024,1024]{1,0:T(8,128)(2,1)}, bf16[1024,1024]{1,0:T(8,128)(2,1)S(1)}, u32[]{:S(2)}) copy-start(bf16[1024,1024]{1,0:T(8,128)(2,1)S(1)} %select_convert_fusion.weights) | copy-start | bytes 6291460
  119.7 57.1 %all-to-all-start.3 = ((bf16[64,16,1024]{2,1,0:T(8,128)(2,1)}), bf16[64,16,1024]{2,1,0:T(8,128)(2,1)}, u32[]{:S(2)}, u32[]{:S(2)}) async-start(bf16[64,16,1024]{2,1,0:T(8,128)(2,1)} %bitcast.64), calls=%async_computation.3 | async-start | bytes 4194304 | tf_op jit(solution)/shard_map/all_to_all | solution.py:21
  176.8 61.3 %all-to-all-start.1 = ((bf16[64,16,1024]{2,1,0:T(8,128)(2,1)}), bf16[64,16,1024]{2,1,0:T(8,128)(2,1)}, u32[]{:S(2)}, u32[]{:S(2)}) async-start(bf16[64,16,1024]{2,1,0:T(8,128)(2,1)} %bitcast.63), calls=%async_computation.1 | async-start | bytes 4194304 | tf_op jit(solution)/shard_map/all_to_all | solution.py:21
  184.9 10.6 %collective-permute-start.10 = (bf16[1024,128]{1,0:T(8,128)(2,1)S(1)}, bf16[1024,128]{1,0:T(8,128)(2,1)S(1)}, u32[]{:S(2)}, u32[]{:S(2)}) collective-permute-start(bf16[1024,128]{1,0:T(8,128)(2,1)S(1)} %add_convert_fusion.5), channel_id=1, source_target_pairs={{64,128},{128,192},{192,0},{65,129},{129,193},{193,1},{66,130},{13... | collective-permute-start | bytes 786440 | tf_op jit(solution)/shard_map/ppermute | solution.py:192
  190.1 30.8 %collective-permute-start.9 = (bf16[1024,512]{1,0:T(8,128)(2,1)}, bf16[1024,512]{1,0:T(8,128)(2,1)S(1)}, u32[]{:S(2)}, u32[]{:S(2)}) collective-permute-start(bf16[1024,512]{1,0:T(8,128)(2,1)} %add_convert_fusion.1), channel_id=1, source_target_pairs={{64,0},{128,64},{192,128},{65,1},{129,65},{193,129},{66,2},{130,66... | collective-permute-start | bytes 3145736 | tf_op jit(solution)/shard_map/ppermute | solution.py:189
  194.1 40.8 %collective-permute-start.8 = (bf16[1024,384]{1,0:T(8,128)(2,1)S(1)}, bf16[1024,384]{1,0:T(8,128)(2,1)S(1)}, u32[]{:S(2)}, u32[]{:S(2)}) collective-permute-start(bf16[1024,384]{1,0:T(8,128)(2,1)S(1)} %add_convert_fusion.3), channel_id=1, source_target_pairs={{64,0},{128,64},{192,128},{65,1},{129,65},{193,129},{66,2},{130,66... | collective-permute-start | bytes 2359304 | tf_op jit(solution)/shard_map/ppermute | solution.py:189
  195.4 13.7 %collective-permute-start.11 = (bf16[1024,128]{1,0:T(8,128)(2,1)S(1)}, bf16[1024,128]{1,0:T(8,128)(2,1)S(1)}, u32[]{:S(2)}, u32[]{:S(2)}) collective-permute-start(bf16[1024,128]{1,0:T(8,128)(2,1)S(1)} %collective-permute-done.10), channel_id=1, source_target_pairs={{128,192},{192,0},{0,64},{129,193},{193,1},{1,65},{130,194},{194,2... | collective-permute-start | bytes 786440 | tf_op jit(solution)/shard_map/ppermute | solution.py:192
  209.1 9.2 %collective-permute-start.12 = (bf16[1024,128]{1,0:T(8,128)(2,1)S(1)}, bf16[1024,128]{1,0:T(8,128)(2,1)S(1)}, u32[]{:S(2)}, u32[]{:S(2)}) collective-permute-start(bf16[1024,128]{1,0:T(8,128)(2,1)S(1)} %collective-permute-done.11), channel_id=1, source_target_pairs={{192,0},{0,64},{64,128},{193,1},{1,65},{65,129},{194,2},{2,66},{66... | collective-permute-start | bytes 786440 | tf_op jit(solution)/shard_map/ppermute | solution.py:192
  238.1 67.6 %all-to-all-start.4 = ((bf16[64,16,1024]{2,1,0:T(8,128)(2,1)}), bf16[64,16,1024]{2,1,0:T(8,128)(2,1)S(1)}, u32[]{:S(2)}, u32[]{:S(2)}) async-start(bf16[64,16,1024]{2,1,0:T(8,128)(2,1)} %bitcast.58), calls=%async_computation.4 | async-start | bytes 4194304 | tf_op jit(solution)/shard_map/all_to_all | solution.py:21
  251.8 12.0 %collective-permute-start.5 = (bf16[1024,128]{1,0:T(8,128)(2,1)S(1)}, bf16[1024,128]{1,0:T(8,128)(2,1)S(1)}, u32[]{:S(2)}, u32[]{:S(2)}) collective-permute-start(bf16[1024,128]{1,0:T(8,128)(2,1)S(1)} %add_convert_fusion.6), channel_id=1, source_target_pairs={{64,128},{128,192},{192,0},{65,129},{129,193},{193,1},{66,130},{13... | collective-permute-start | bytes 786440 | tf_op jit(solution)/shard_map/ppermute | solution.py:192
  257.7 31.3 %collective-permute-start.4 = (bf16[1024,512]{1,0:T(8,128)(2,1)}, bf16[1024,512]{1,0:T(8,128)(2,1)}, u32[]{:S(2)}, u32[]{:S(2)}) collective-permute-start(bf16[1024,512]{1,0:T(8,128)(2,1)} %add_convert_fusion.2), channel_id=1, source_target_pairs={{64,0},{128,64},{192,128},{65,1},{129,65},{193,129},{66,2},{130,66... | collective-permute-start | bytes 3145736 | tf_op jit(solution)/shard_map/ppermute | solution.py:189
  262.6 39.9 %collective-permute-start.3 = (bf16[1024,384]{1,0:T(8,128)(2,1)}, bf16[1024,384]{1,0:T(8,128)(2,1)S(1)}, u32[]{:S(2)}, u32[]{:S(2)}) collective-permute-start(bf16[1024,384]{1,0:T(8,128)(2,1)} %add_convert_fusion.4), channel_id=1, source_target_pairs={{64,0},{128,64},{192,128},{65,1},{129,65},{193,129},{66,2},{130,66... | collective-permute-start | bytes 2359304 | tf_op jit(solution)/shard_map/ppermute | solution.py:189
  263.9 13.6 %collective-permute-start.6 = (bf16[1024,128]{1,0:T(8,128)(2,1)S(1)}, bf16[1024,128]{1,0:T(8,128)(2,1)S(1)}, u32[]{:S(2)}, u32[]{:S(2)}) collective-permute-start(bf16[1024,128]{1,0:T(8,128)(2,1)S(1)} %collective-permute-done.5), channel_id=1, source_target_pairs={{128,192},{192,0},{0,64},{129,193},{193,1},{1,65},{130,194},{194,2... | collective-permute-start | bytes 786440 | tf_op jit(solution)/shard_map/ppermute | solution.py:192
  277.5 9.1 %collective-permute-start.7 = (bf16[1024,128]{1,0:T(8,128)(2,1)S(1)}, bf16[1024,128]{1,0:T(8,128)(2,1)S(1)}, u32[]{:S(2)}, u32[]{:S(2)}) collective-permute-start(bf16[1024,128]{1,0:T(8,128)(2,1)S(1)} %collective-permute-done.6), channel_id=1, source_target_pairs={{192,0},{0,64},{64,128},{193,1},{1,65},{65,129},{194,2},{2,66},{66... | collective-permute-start | bytes 786440 | tf_op jit(solution)/shard_map/ppermute | solution.py:192
  305.7 62.6 %all-to-all-start.2 = ((bf16[64,16,1024]{2,1,0:T(8,128)(2,1)}), bf16[64,16,1024]{2,1,0:T(8,128)(2,1)}, u32[]{:S(2)}, u32[]{:S(2)}) async-start(bf16[64,16,1024]{2,1,0:T(8,128)(2,1)} %bitcast.57), calls=%async_computation.2 | async-start | bytes 4194304 | tf_op jit(solution)/shard_map/all_to_all | solution.py:21
  373.7 102.0 %all-to-all-start.5 = ((bf16[64,16,2048]{2,1,0:T(8,128)(2,1)}), bf16[64,16,2048]{2,1,0:T(8,128)(2,1)}, u32[]{:S(2)}, u32[]{:S(2)}) async-start(bf16[64,16,2048]{2,1,0:T(8,128)(2,1)} %bitcast.56), calls=%async_computation.5 | async-start | bytes 8388608 | tf_op jit(solution)/shard_map/all_to_all | solution.py:21
  379.9 13.2 %collective-permute-start.15 = (bf16[1024,128]{1,0:T(8,128)(2,1)}, bf16[1024,128]{1,0:T(8,128)(2,1)S(1)}, u32[]{:S(2)}, u32[]{:S(2)}) collective-permute-start(bf16[1024,128]{1,0:T(8,128)(2,1)} %copy-done.28), channel_id=1, source_target_pairs={{0,128},{1,129},{2,130},{3,131},{4,132},{5,133},{6,134},{7,135},{8... | collective-permute-start | bytes 786440 | tf_op jit(solution)/shard_map/ppermute | solution.py:221
  383.7 22.3 %collective-permute-start.14 = (bf16[1024,384]{1,0:T(8,128)(2,1)}, bf16[1024,384]{1,0:T(8,128)(2,1)S(1)}, u32[]{:S(2)}, u32[]{:S(2)}) collective-permute-start(bf16[1024,384]{1,0:T(8,128)(2,1)} %add_convert_fusion.4), channel_id=1, source_target_pairs={{0,128},{1,129},{2,130},{3,131},{4,132},{5,133},{6,134},{7,135},{8... | collective-permute-start | bytes 2359304 | tf_op jit(solution)/shard_map/ppermute | solution.py:221
  385.1 43.4 %collective-permute-start.16 = (bf16[1024,512]{1,0:T(8,128)(2,1)}, bf16[1024,512]{1,0:T(8,128)(2,1)S(1)}, u32[]{:S(2)}, u32[]{:S(2)}) collective-permute-start(bf16[1024,512]{1,0:T(8,128)(2,1)} %add_convert_fusion.1), channel_id=1, source_target_pairs={{0,64},{1,65},{2,66},{3,67},{4,68},{5,69},{6,70},{7,71},{8,72},{9,... | collective-permute-start | bytes 3145736 | tf_op jit(solution)/shard_map/ppermute | solution.py:221
  386.6 41.8 %collective-permute-start.13 = (bf16[1024,512]{1,0:T(8,128)(2,1)}, bf16[1024,512]{1,0:T(8,128)(2,1)S(1)}, u32[]{:S(2)}, u32[]{:S(2)}) collective-permute-start(bf16[1024,512]{1,0:T(8,128)(2,1)} %add_convert_fusion.2), channel_id=1, source_target_pairs={{0,192},{1,193},{2,194},{3,195},{4,196},{5,197},{6,198},{7,199},{8... | collective-permute-start | bytes 3145736 | tf_op jit(solution)/shard_map/ppermute | solution.py:221
  (28 other events, 467.6 us)

commit v3 on v2

--- a/solution.py
+++ b/solution.py
@@ -56,6 +56,35 @@
             flops=2 * rows * (rows // count) * channels, bytes_accessed=4 * rows * channels, transcendentals=0
         ),
     )(*operands)
+
+
+def restore_kernel(count, rows_in, rows_out):
+    order = rows_in.shape[0] // count
+    chunk, tile = order // count, count * count
+    m = lax.broadcasted_iota(jnp.int32, (order, order), 0)
+    n = lax.broadcasted_iota(jnp.int32, (order, order), 1)
+    place = (m == (n // count % count) * chunk + (n // tile) * count + n % count).astype(BF16)
+    for group in range(count):
+        placed = dot(place, rows_in[group * order:(group + 1) * order, :]).astype(BF16)
+        for il in range(count):
+            start = il * order + group * chunk
+            rows_out[start:start + chunk, :] = placed[il * chunk:(il + 1) * chunk, :]
+
+
+def restore(rows_in, count):
+    rows, channels = rows_in.shape
+    width = min(1024, channels)
+    block = pl.BlockSpec((rows, width), lambda n: (0, n))
+    return pl.pallas_call(
+        functools.partial(restore_kernel, count),
+        out_shape=jax.ShapeDtypeStruct(rows_in.shape, BF16),
+        grid=(channels // width,),
+        in_specs=[block],
+        out_specs=block,
+        cost_estimate=pl.CostEstimate(
+            flops=2 * rows * (rows // count) * channels, bytes_accessed=4 * rows * channels, transcendentals=0
+        ),
+    )(rows_in)
 
 
 def scale_kernel(flag, gain, here, moved, *rest):
@@ -94,13 +123,14 @@
     rest[-1][...] = dot(weights[...], columns[...]).astype(BF16)
 
 
-def product_into(weights, columns, total, at, buffer=None):
+def product_into(weights, columns, taken, total, at, buffer=None):
     rows, depth = weights.shape
-    width = min(512, columns.shape[1])
-    steps, first = columns.shape[1] // width, at // width
+    count = taken.stop - taken.start
+    width = min(512, count)
+    steps, source, first = count // width, taken.start // width, at // width
     in_specs = [
         pl.BlockSpec((rows, depth), lambda n: (0, 0), pipeline_mode=pl.Buffered(1)),
-        pl.BlockSpec((depth, width), lambda n: (0, n)),
+        pl.BlockSpec((depth, width), lambda n: (0, source + n)),
     ]
     operands = [weights, columns]
     aliases = {}
@@ -116,8 +146,8 @@
         out_specs=pl.BlockSpec((rows, width), lambda n: (0, first + n)),
         input_output_aliases=aliases,
         cost_estimate=pl.CostEstimate(
-            flops=2 * rows * depth * columns.shape[1],
-            bytes_accessed=2 * (rows * depth + 2 * rows * columns.shape[1]),
+            flops=2 * rows * depth * count,
+            bytes_accessed=2 * (rows * depth + 2 * rows * count),
             transcendentals=0,
         ),
     )(*operands)
@@ -136,7 +166,6 @@
 
     out = lax.broadcasted_iota(jnp.int32, (rows, rows), 0)
     into = lax.broadcasted_iota(jnp.int32, (rows, rows), 1)
-    natural = (out // count % count) * order + (out // tile) * count + out % count
 
     at = lax.broadcasted_iota(jnp.int32, (count, rows, order), 1)
     col = lax.broadcasted_iota(jnp.int32, (count, rows, order), 2)
@@ -153,11 +182,7 @@
     first_spread = jnp.where(out // order == into // count % count, wide, 0.0).astype(BF16)
 
     inner, outer = inner_gain, outer_gain.astype(F32)
-    restore = (natural.T == into.T).astype(BF16)
     first_sent = reorder(first_spread, count)
-
-    def mix(columns):
-        return dot(second_spread, columns).astype(BF16)
 
     def finish(gradient, weights, returned, cols):
         spread = dot(weights, returned)
@@ -172,8 +197,13 @@
     reordered = reorder(arriving[0], count)
     loss_sent = reorder(loss_grad, count)
     lost = [loss_sent if q == last else lax.ppermute(loss_sent, "pipe", [(q, last)]) for q in range(sections)]
-    around = piece // sections
-    cuts = ((0, piece - around, False), (piece - around, around, True), (piece, piece, False))
+    around = piece // 4
+    cuts = (
+        (0, 2 * around, False),
+        (2 * around, around, True),
+        (3 * around, around, True),
+        (piece, piece, False),
+    )
     here = [
         [lost[n * per_half + start // piece][:, start % piece:start % piece + width] for start, width, _ in cuts]
         for n in range(2)
@@ -181,7 +211,7 @@
     columns, here, first_sent, reordered = lax.optimization_barrier((first_sending, here, first_sent, reordered))
 
     back = [(i + 1, i) for i in range(sections - 1)]
-    returned = [exchange(mix(columns[:, h]), devices) for h in halves]
+    returned = [exchange(product_into(second_spread, columns, h, channels // 2, 0), devices) for h in halves]
     flag = (position == last).astype(jnp.int32).reshape(1)
 
     def shift(block, round_about):
@@ -202,8 +232,7 @@
 
     def fill(n, moved):
         buffer = None
-        for c in (1, 2, 0):
-            start, width, _ = cuts[c]
+        for c, (start, width, _) in enumerate(cuts):
             gain = inner[:, halves[n].start + start:halves[n].start + start + width]
             buffer = scale_into(flag, gain, here[n][c], moved[c], channels // 2, start, buffer)
         return buffer
@@ -215,18 +244,18 @@
         passed.append(done)
         moved += shifted
 
-    leaving = jnp.concatenate(passed[0][:2], axis=1)
+    leaving = jnp.concatenate(passed[0][:-1], axis=1)
     for q in range(1, sections):
-        parts = passed[q // per_half][:2] if q % per_half == 0 else passed[q // per_half][2:]
-        parts = jnp.concatenate([lax.ppermute(p, "pipe", [(0, q)]) for p in parts], axis=1)
+        parts = passed[q // per_half][:-1] if q % per_half == 0 else passed[q // per_half][-1:]
+        parts = lax.ppermute(jnp.concatenate(parts, axis=1), "pipe", [(0, q)])
         leaving = jnp.where(position == q, parts, leaving)
-    leaving = dot(restore, leaving).astype(BF16)
-
-    mixed = product_into(second_spread, sent[0], channels, 0)
-    mixed = product_into(second_spread, sent[1], channels, channels // 2, mixed)
+    leaving = restore(leaving, count)
+
+    mixed = product_into(second_spread, sent[0], slice(0, channels // 2), channels, 0)
+    mixed = product_into(second_spread, sent[1], slice(0, channels // 2), channels, channels // 2, mixed)
     final = exchange(mixed, devices)
     source = jnp.concatenate([jnp.where(position == last, a, b) for a, b in zip(here[0] + here[1], moved)], axis=1)
-    source = dot(restore, source).astype(BF16)
+    source = restore(source, count)
     final, source, leaving = lax.optimization_barrier((final, source, leaving))
     entering = finish(source, first_spread, final, whole)
     return entering[None], leaving

time: 486 us -> 502 us (1.033)
  Pallas kernels: 39.4 us -> 60.7 us
  matrix products: 49.8 us -> 30 us
  other arithmetic: 7.45 us -> 21.5 us
  waiting for transfers between devices: 278 us -> 269 us
  starting transfers between devices: 94.4 us -> 102 us
    dot_general x12 -> x10, matrix products: 49 us -> 29.2 us  [dot(): lax.dot_general(a, b, (((1,), (0,)), ((), ())), preferred_element_type=F32)]
    pallas_call x2 -> x4, Pallas kernels: 10.8 us -> 21.8 us  [product_into(): pl.pallas_call(product_kernel, out_shape=jax.ShapeDtypeStruct((rows, tota...]
    all_to_all x6, waiting for transfers between devices: 168 us -> 159 us  [exchange(): blocks = lax.all_to_all(blocks, 'seq', split_axis=0, concat_axis=0)]
    pallas_call x0 -> x2, Pallas kernels: none -> 7.34 us  [restore(): pl.pallas_call(functools.partial(restore_kernel, count), out_shape=jax.Sh...]
    broadcast_in_dim x0 -> x1, other arithmetic: none -> 6.94 us  [local_program(): return (entering[None], leaving)]
    ppermute x6 -> x12, starting transfers between devices: 18.8 us -> 25.1 us  [shift(): block = lax.ppermute(block, 'pipe', route)]
    ppermute x6 -> x12, waiting for transfers between devices: 27.7 us -> 24.2 us  [shift(): block = lax.ppermute(block, 'pipe', route)]
    pallas_call x6 -> x8, Pallas kernels: 13.3 us -> 16.3 us  [scale_into(): pl.pallas_call(scale_kernel, out_shape=jax.ShapeDtypeStruct((rows, total)...]
  transfers between devices with their start and end apart: 23 -> 28, of which waited for: 13 -> 16; matrix products, arithmetic and copies ran while one was open for 11% -> 9% of each run, Pallas kernels for 6% -> 9%
where the time goes in v3:
time: 502 us; the launch traced here: 500 us
  waiting for transfers between devices  269 us (54%)
  starting transfers between devices  102 us (20%)
  Pallas kernels  60.7 us (12%)
  matrix products  30 us (6%)
  other arithmetic  21.5 us (4%)
  local copies, waits for them, and re-layouts  15.4 us (3%)
    all_to_all x6, waiting for transfers between devices, exchange(): blocks = lax.all_to_all(blocks, 'seq', split_axis=0, concat_axis=0)  159 us
    all_to_all x6, starting transfers between devices, exchange(): blocks = lax.all_to_all(blocks, 'seq', split_axis=0, concat_axis=0)  54.3 us
    ppermute x3, waiting for transfers between devices, local_program(): parts = lax.ppermute(jnp.concatenate(parts, axis=1), 'pipe', [(0, q)])  36.1 us
    dot_general x10, matrix products, dot(): lax.dot_general(a, b, (((1,), (0,)), ((), ())), preferred_element_type=F32)  29.2 us
    ppermute x3, waiting for transfers between devices, local_program(): lax.ppermute(loss_sent, 'pipe', [(q, last)])  27.8 us
    ppermute x12, starting transfers between devices, shift(): block = lax.ppermute(block, 'pipe', route)  25.1 us
    ppermute x12, waiting for transfers between devices, shift(): block = lax.ppermute(block, 'pipe', route)  24.2 us
    ppermute x4, waiting for transfers between devices, shift(): return lax.ppermute(block, 'pipe', back)  22.2 us
  transfers between devices with their start and end apart: 28, of which 16 were waited for; matrix products, arithmetic and copies ran while one was open for 9% of the time, Pallas kernels for 9%

profile of v3, /device:TPU:1, one launch (start us, length us, event | category | flops | bytes accessed | tf_op | source)
XLA Modules:
  0.0 500.4 jit_solution(13146707516224266610)
XLA Ops:
  5.3 13.3 %all-to-all-start = ((bf16[64,16,2048]{2,1,0:T(8,128)(2,1)}), bf16[64,16,2048]{2,1,0:T(8,128)(2,1)}, u32[]{:S(2)}, u32[]{:S(2)}) async-start(bf16[64,16,2048]{2,1,0:T(8,128)(2,1)} %bitcast.66), calls=%async_computation | async-start | bytes 8388608 | tf_op jit(solution)/shard_map/all_to_all | solution.py:21
  22.7 6.5 %collective-permute-start = (bf16[1024,512]{1,0:T(8,128)(2,1)}, bf16[1024,512]{1,0:T(8,128)(2,1)}, u32[]{:S(2)}, u32[]{:S(2)}) collective-permute-start(bf16[1024,512]{1,0:T(8,128)(2,1)} %shard_map.78.here), channel_id=1, source_target_pairs={{0,192},{1,193},{2,194},{3,195},{4,196},{5,197},{6,198},{7,199},{8... | collective-permute-start | bytes 3145736 | tf_op jit(solution)/shard_map/ppermute | solution.py:199
  45.1 27.8 %collective-permute-done = bf16[1024,512]{1,0:T(8,128)(2,1)} collective-permute-done((bf16[1024,512]{1,0:T(8,128)(2,1)}, bf16[1024,512]{1,0:T(8,128)(2,1)}, u32[]{:S(2)}, u32[]{:S(2)}) %collective-permute-start) | collective-permute-done | bytes 1048608 | tf_op jit(solution)/shard_map/ppermute | solution.py:199
  77.4 37.0 %all-to-all-done = bf16[64,16,2048]{2,1,0:T(8,128)(2,1)} async-done(((bf16[64,16,2048]{2,1,0:T(8,128)(2,1)}), bf16[64,16,2048]{2,1,0:T(8,128)(2,1)}, u32[]{:S(2)}, u32[]{:S(2)}) %all-to-all-start) | async-done | bytes 4194336 | tf_op jit(solution)/shard_map/all_to_all | solution.py:21
  114.5 5.5 %shard_map.86 = bf16[1024,1024]{1,0:T(8,128)(2,1)} custom-call(bf16[1024,1024]{1,0:T(8,128)(2,1)} %select_convert_fusion.weights, bf16[1024,2048]{1,0:T(8,128)(2,1)} %bitcast.5.columns), custom_call_target="tpu_custom_call" | custom-call | flops 2147483648 | bytes 6291456 | tf_op jit(solution)/shard_map/pallas_call | solution.py:141
  120.0 5.7 %all-to-all-start.3 = ((bf16[64,16,1024]{2,1,0:T(8,128)(2,1)}), bf16[64,16,1024]{2,1,0:T(8,128)(2,1)S(1)}, u32[]{:S(2)}, u32[]{:S(2)}) async-start(bf16[64,16,1024]{2,1,0:T(8,128)(2,1)} %bitcast.69), calls=%async_computation.3 | async-start | bytes 4194304 | tf_op jit(solution)/shard_map/all_to_all | solution.py:21
  125.7 5.4 %shard_map.81 = bf16[1024,1024]{1,0:T(8,128)(2,1)} custom-call(bf16[1024,1024]{1,0:T(8,128)(2,1)} %select_convert_fusion.weights, bf16[1024,2048]{1,0:T(8,128)(2,1)} %bitcast.5.columns), custom_call_target="tpu_custom_call" | custom-call | flops 2147483648 | bytes 6291456 | tf_op jit(solution)/shard_map/pallas_call | solution.py:141
  131.2 45.8 %all-to-all-done.3 = bf16[64,16,1024]{2,1,0:T(8,128)(2,1)S(1)} async-done(((bf16[64,16,1024]{2,1,0:T(8,128)(2,1)}), bf16[64,16,1024]{2,1,0:T(8,128)(2,1)S(1)}, u32[]{:S(2)}, u32[]{:S(2)}) %all-to-all-start.3) | async-done | bytes 2097184 | tf_op jit(solution)/shard_map/all_to_all | solution.py:21
  178.3 6.2 %all-to-all-start.1 = ((bf16[64,16,1024]{2,1,0:T(8,128)(2,1)}), bf16[64,16,1024]{2,1,0:T(8,128)(2,1)}, u32[]{:S(2)}, u32[]{:S(2)}) async-start(bf16[64,16,1024]{2,1,0:T(8,128)(2,1)} %bitcast.67), calls=%async_computation.1 | async-start | bytes 4194304 | tf_op jit(solution)/shard_map/all_to_all | solution.py:21
  217.4 16.5 %collective-permute-done.18.moved = bf16[1024,256]{1,0:T(8,128)(2,1)S(1)} collective-permute-done((bf16[1024,256]{1,0:T(8,128)(2,1)S(1)}, bf16[1024,256]{1,0:T(8,128)(2,1)S(1)}, u32[]{:S(2)}, u32[]{:S(2)}) %collective-permute-start.18) | collective-permute-done | bytes 524320 | tf_op jit(solution)/shard_map/ppermute | solution.py:219
  245.2 11.5 %all-to-all-start.4 = ((bf16[64,16,1024]{2,1,0:T(8,128)(2,1)}), bf16[64,16,1024]{2,1,0:T(8,128)(2,1)S(1)}, u32[]{:S(2)}, u32[]{:S(2)}) async-start(bf16[64,16,1024]{2,1,0:T(8,128)(2,1)} %bitcast.61), calls=%async_computation.4 | async-start | bytes 4194304 | tf_op jit(solution)/shard_map/all_to_all | solution.py:21
  272.0 7.8 %collective-permute-done.7 = bf16[1024,128]{1,0:T(8,128)(2,1)S(1)} collective-permute-done((bf16[1024,128]{1,0:T(8,128)(2,1)S(1)}, bf16[1024,128]{1,0:T(8,128)(2,1)S(1)}, u32[]{:S(2)}, u32[]{:S(2)}) %collective-permute-start.7) | collective-permute-done | bytes 262176 | tf_op jit(solution)/shard_map/ppermute | solution.py:222
  283.6 5.8 %collective-permute-done.8 = bf16[1024,128]{1,0:T(8,128)(2,1)S(1)} collective-permute-done((bf16[1024,128]{1,0:T(8,128)(2,1)S(1)}, bf16[1024,128]{1,0:T(8,128)(2,1)S(1)}, u32[]{:S(2)}, u32[]{:S(2)}) %collective-permute-start.8) | collective-permute-done | bytes 262176 | tf_op jit(solution)/shard_map/ppermute | solution.py:222
  297.0 5.7 %collective-permute-done.10.moved = bf16[1024,256]{1,0:T(8,128)(2,1)S(1)} collective-permute-done((bf16[1024,256]{1,0:T(8,128)(2,1)S(1)}, bf16[1024,256]{1,0:T(8,128)(2,1)S(1)}, u32[]{:S(2)}, u32[]{:S(2)}) %collective-permute-start.10) | collective-permute-done | bytes 524320 | tf_op jit(solution)/shard_map/ppermute | solution.py:219
  314.5 11.4 %all-to-all-start.2 = ((bf16[64,16,1024]{2,1,0:T(8,128)(2,1)}), bf16[64,16,1024]{2,1,0:T(8,128)(2,1)}, u32[]{:S(2)}, u32[]{:S(2)}) async-start(bf16[64,16,1024]{2,1,0:T(8,128)(2,1)} %bitcast.62), calls=%async_computation.2 | async-start | bytes 4194304 | tf_op jit(solution)/shard_map/all_to_all | solution.py:21
  325.9 5.4 %shard_map.91.rest_0_ = bf16[1024,2048]{1,0:T(8,128)(2,1)} custom-call(bf16[1024,1024]{1,0:T(8,128)(2,1)} %select_convert_fusion.weights, bf16[1024,1024]{1,0:T(8,128)(2,1)} %bitcast.68), custom_call_target="tpu_custom_call" | custom-call | flops 2147483648 | bytes 6291456 | tf_op jit(solution)/shard_map/pallas_call | solution.py:141
  331.3 45.7 %all-to-all-done.2 = bf16[64,16,1024]{2,1,0:T(8,128)(2,1)} async-done(((bf16[64,16,1024]{2,1,0:T(8,128)(2,1)}), bf16[64,16,1024]{2,1,0:T(8,128)(2,1)}, u32[]{:S(2)}, u32[]{:S(2)}) %all-to-all-start.2) | async-done | bytes 2097184 | tf_op jit(solution)/shard_map/all_to_all | solution.py:21
  377.0 5.4 %shard_map.92 = bf16[1024,2048]{1,0:T(8,128)(2,1)} custom-call(bf16[1024,1024]{1,0:T(8,128)(2,1)} %select_convert_fusion.weights, bf16[1024,1024]{1,0:T(8,128)(2,1)} %bitcast.17.columns, bf16[1024,2048]{1,0:T(8,128)(2,1)} %shard_map.91.rest_0_), custom_call_target="tpu_custom_call", output_to_operand_aliasing={{}: (2, {})} | custom-call | flops 2147483648 | bytes 6291456 | tf_op jit(solution)/shard_map/pallas_call | solution.py:141
  382.4 6.2 %all-to-all-start.5 = ((bf16[64,16,2048]{2,1,0:T(8,128)(2,1)}), bf16[64,16,2048]{2,1,0:T(8,128)(2,1)}, u32[]{:S(2)}, u32[]{:S(2)}) async-start(bf16[64,16,2048]{2,1,0:T(8,128)(2,1)} %bitcast.63), calls=%async_computation.5 | async-start | bytes 8388608 | tf_op jit(solution)/shard_map/all_to_all | solution.py:21
  402.3 13.5 %collective-permute-done.20 = bf16[1024,512]{1,0:T(8,128)(2,1)} collective-permute-done((bf16[1024,512]{1,0:T(8,128)(2,1)S(1)}, bf16[1024,512]{1,0:T(8,128)(2,1)}, u32[]{:S(2)}, u32[]{:S(2)}) %collective-permute-start.20) | collective-permute-done | bytes 1048608 | tf_op jit(solution)/shard_map/ppermute | solution.py:250
  415.8 22.6 %collective-permute-done.21 = bf16[1024,512]{1,0:T(8,128)(2,1)} collective-permute-done((bf16[1024,512]{1,0:T(8,128)(2,1)}, bf16[1024,512]{1,0:T(8,128)(2,1)}, u32[]{:S(2)}, u32[]{:S(2)}) %collective-permute-start.21) | collective-permute-done | bytes 1048608 | tf_op jit(solution)/shard_map/ppermute | solution.py:250
  454.0 30.5 %all-to-all-done.5 = bf16[64,16,2048]{2,1,0:T(8,128)(2,1)} async-done(((bf16[64,16,2048]{2,1,0:T(8,128)(2,1)}), bf16[64,16,2048]{2,1,0:T(8,128)(2,1)}, u32[]{:S(2)}, u32[]{:S(2)}) %all-to-all-start.5) | async-done | bytes 4194336 | tf_op jit(solution)/shard_map/all_to_all | solution.py:21
  484.5 9.0 %fusion.64 = f32[1024,2048]{1,0:T(8,128)} fusion(bf16[1024,1024]{1,0:T(8,128)(2,1)S(1)} %copy-done.4, bf16[1024,2048]{1,0:T(8,128)(2,1)} %bitcast.27), kind=kOutput, calls=%fused_computation.101 | convolution fusion | flops 4294967296 | bytes 14680064 | tf_op jit(solution)/shard_map/dot_general | solution.py:15
  493.5 6.9 %fusion.2 = bf16[1,1024,2048]{2,1,0:T(8,128)(2,1)} fusion(f32[1024,2048]{1,0:T(8,128)} %fusion.64, bf16[1024,2048]{1,0:T(8,128)(2,1)S(1)} %copy-done.2, f32[2048]{0:T(1024)S(1)} %bitcast.74), kind=kLoop, calls=%fused_computation.8 | loop fusion | flops 8388608 | bytes 16785408 | tf_op jit(solution)/shard_map/broadcast_in_dim | solution.py:261
  (186 shorter events, 142.0 us)
Async XLA Ops:
  5.3 109.2 %all-to-all-start = ((bf16[64,16,2048]{2,1,0:T(8,128)(2,1)}), bf16[64,16,2048]{2,1,0:T(8,128)(2,1)}, u32[]{:S(2)}, u32[]{:S(2)}) async-start(bf16[64,16,2048]{2,1,0:T(8,128)(2,1)} %bitcast.66), calls=%async_computation | async-start | bytes 8388608 | tf_op jit(solution)/shard_map/all_to_all | solution.py:21
  21.2 23.0 %collective-permute-start.2 = (bf16[1024,512]{1,0:T(8,128)(2,1)}, bf16[1024,512]{1,0:T(8,128)(2,1)S(1)}, u32[]{:S(2)}, u32[]{:S(2)}) collective-permute-start(bf16[1024,512]{1,0:T(8,128)(2,1)} %shard_map.78.here), channel_id=1, source_target_pairs={{128,192},{129,193},{130,194},{131,195},{132,196},{133,197},{134,1... | collective-permute-start | bytes 3145736 | tf_op jit(solution)/shard_map/ppermute | solution.py:199
  22.0 55.5 %collective-permute-start.1 = (bf16[1024,512]{1,0:T(8,128)(2,1)}, bf16[1024,512]{1,0:T(8,128)(2,1)S(1)}, u32[]{:S(2)}, u32[]{:S(2)}) collective-permute-start(bf16[1024,512]{1,0:T(8,128)(2,1)} %shard_map.78.here), channel_id=1, source_target_pairs={{64,192},{65,193},{66,194},{67,195},{68,196},{69,197},{70,198},{71... | collective-permute-start | bytes 3145736 | tf_op jit(solution)/shard_map/ppermute | solution.py:199
  22.7 50.2 %collective-permute-start = (bf16[1024,512]{1,0:T(8,128)(2,1)}, bf16[1024,512]{1,0:T(8,128)(2,1)}, u32[]{:S(2)}, u32[]{:S(2)}) collective-permute-start(bf16[1024,512]{1,0:T(8,128)(2,1)} %shard_map.78.here), channel_id=1, source_target_pairs={{0,192},{1,193},{2,194},{3,195},{4,196},{5,197},{6,198},{7,199},{8... | collective-permute-start | bytes 3145736 | tf_op jit(solution)/shard_map/ppermute | solution.py:199
  120.0 57.0 %all-to-all-start.3 = ((bf16[64,16,1024]{2,1,0:T(8,128)(2,1)}), bf16[64,16,1024]{2,1,0:T(8,128)(2,1)S(1)}, u32[]{:S(2)}, u32[]{:S(2)}) async-start(bf16[64,16,1024]{2,1,0:T(8,128)(2,1)} %bitcast.69), calls=%async_computation.3 | async-start | bytes 4194304 | tf_op jit(solution)/shard_map/all_to_all | solution.py:21
  178.3 66.9 %all-to-all-start.1 = ((bf16[64,16,1024]{2,1,0:T(8,128)(2,1)}), bf16[64,16,1024]{2,1,0:T(8,128)(2,1)}, u32[]{:S(2)}, u32[]{:S(2)}) async-start(bf16[64,16,1024]{2,1,0:T(8,128)(2,1)} %bitcast.67), calls=%async_computation.1 | async-start | bytes 4194304 | tf_op jit(solution)/shard_map/all_to_all | solution.py:21
  189.7 13.0 %collective-permute-start.15 = (bf16[1024,128]{1,0:T(8,128)(2,1)S(1)}, bf16[1024,128]{1,0:T(8,128)(2,1)S(1)}, u32[]{:S(2)}, u32[]{:S(2)}) collective-permute-start(bf16[1024,128]{1,0:T(8,128)(2,1)S(1)} %add_convert_fusion.5), channel_id=1, source_target_pairs={{64,128},{128,192},{192,0},{65,129},{129,193},{193,1},{66,130},{13... | collective-permute-start | bytes 786440 | tf_op jit(solution)/shard_map/ppermute | solution.py:222
  193.4 48.3 %collective-permute-start.11 = (bf16[1024,512]{1,0:T(8,128)(2,1)}, bf16[1024,512]{1,0:T(8,128)(2,1)S(1)}, u32[]{:S(2)}, u32[]{:S(2)}) collective-permute-start(bf16[1024,512]{1,0:T(8,128)(2,1)} %add_convert_fusion.1), channel_id=1, source_target_pairs={{64,0},{128,64},{192,128},{65,1},{129,65},{193,129},{66,2},{130,66... | collective-permute-start | bytes 3145736 | tf_op jit(solution)/shard_map/ppermute | solution.py:219
  205.4 28.4 %collective-permute-start.18 = (bf16[1024,256]{1,0:T(8,128)(2,1)S(1)}, bf16[1024,256]{1,0:T(8,128)(2,1)S(1)}, u32[]{:S(2)}, u32[]{:S(2)}) collective-permute-start(bf16[1024,256]{1,0:T(8,128)(2,1)S(1)} %add_convert_fusion.3), channel_id=1, source_target_pairs={{64,0},{128,64},{192,128},{65,1},{129,65},{193,129},{66,2},{130,66... | collective-permute-start | bytes 1572872 | tf_op jit(solution)/shard_map/ppermute | solution.py:219
  207.9 31.3 %collective-permute-start.14 = (bf16[1024,128]{1,0:T(8,128)(2,1)S(1)}, bf16[1024,128]{1,0:T(8,128)(2,1)S(1)}, u32[]{:S(2)}, u32[]{:S(2)}) collective-permute-start(bf16[1024,128]{1,0:T(8,128)(2,1)S(1)} %collective-permute-done.13), channel_id=1, source_target_pairs={{192,0},{0,64},{64,128},{193,1},{1,65},{65,129},{194,2},{2,66},{66... | collective-permute-start | bytes 786440 | tf_op jit(solution)/shard_map/ppermute | solution.py:222
  214.2 22.4 %collective-permute-start.17 = (bf16[1024,128]{1,0:T(8,128)(2,1)}, bf16[1024,128]{1,0:T(8,128)(2,1)S(1)}, u32[]{:S(2)}, u32[]{:S(2)}) collective-permute-start(bf16[1024,128]{1,0:T(8,128)(2,1)} %collective-permute-done.16), channel_id=1, source_target_pairs={{192,0},{0,64},{64,128},{193,1},{1,65},{65,129},{194,2},{2,66},{66... | collective-permute-start | bytes 786440 | tf_op jit(solution)/shard_map/ppermute | solution.py:222
  245.2 67.9 %all-to-all-start.4 = ((bf16[64,16,1024]{2,1,0:T(8,128)(2,1)}), bf16[64,16,1024]{2,1,0:T(8,128)(2,1)S(1)}, u32[]{:S(2)}, u32[]{:S(2)}) async-start(bf16[64,16,1024]{2,1,0:T(8,128)(2,1)} %bitcast.61), calls=%async_computation.4 | async-start | bytes 4194304 | tf_op jit(solution)/shard_map/all_to_all | solution.py:21
  259.3 22.4 %collective-permute-start.4 = (bf16[1024,128]{1,0:T(8,128)(2,1)S(1)}, bf16[1024,128]{1,0:T(8,128)(2,1)S(1)}, u32[]{:S(2)}, u32[]{:S(2)}) collective-permute-start(bf16[1024,128]{1,0:T(8,128)(2,1)S(1)} %add_convert_fusion.8), channel_id=1, source_target_pairs={{64,128},{128,192},{192,0},{65,129},{129,193},{193,1},{66,130},{13... | collective-permute-start | bytes 786440 | tf_op jit(solution)/shard_map/ppermute | solution.py:222
  264.4 46.2 %collective-permute-start.3 = (bf16[1024,512]{1,0:T(8,128)(2,1)}, bf16[1024,512]{1,0:T(8,128)(2,1)}, u32[]{:S(2)}, u32[]{:S(2)}) collective-permute-start(bf16[1024,512]{1,0:T(8,128)(2,1)} %add_convert_fusion.2), channel_id=1, source_target_pairs={{64,0},{128,64},{192,128},{65,1},{129,65},{193,129},{66,2},{130,66... | collective-permute-start | bytes 3145736 | tf_op jit(solution)/shard_map/ppermute | solution.py:219
  267.4 12.3 %collective-permute-start.7 = (bf16[1024,128]{1,0:T(8,128)(2,1)S(1)}, bf16[1024,128]{1,0:T(8,128)(2,1)S(1)}, u32[]{:S(2)}, u32[]{:S(2)}) collective-permute-start(bf16[1024,128]{1,0:T(8,128)(2,1)S(1)} %add_convert_fusion.7), channel_id=1, source_target_pairs={{64,128},{128,192},{192,0},{65,129},{129,193},{193,1},{66,130},{13... | collective-permute-start | bytes 786440 | tf_op jit(solution)/shard_map/ppermute | solution.py:222
  270.7 32.1 %collective-permute-start.10 = (bf16[1024,256]{1,0:T(8,128)(2,1)S(1)}, bf16[1024,256]{1,0:T(8,128)(2,1)S(1)}, u32[]{:S(2)}, u32[]{:S(2)}) collective-permute-start(bf16[1024,256]{1,0:T(8,128)(2,1)S(1)} %add_convert_fusion.4), channel_id=1, source_target_pairs={{64,0},{128,64},{192,128},{65,1},{129,65},{193,129},{66,2},{130,66... | collective-permute-start | bytes 1572872 | tf_op jit(solution)/shard_map/ppermute | solution.py:219
  281.7 13.4 %collective-permute-start.5 = (bf16[1024,128]{1,0:T(8,128)(2,1)S(1)}, bf16[1024,128]{1,0:T(8,128)(2,1)}, u32[]{:S(2)}, u32[]{:S(2)}) collective-permute-start(bf16[1024,128]{1,0:T(8,128)(2,1)S(1)} %collective-permute-done.4), channel_id=1, source_target_pairs={{128,192},{192,0},{0,64},{129,193},{193,1},{1,65},{130,194},{194,2... | collective-permute-start | bytes 786440 | tf_op jit(solution)/shard_map/ppermute | solution.py:222
  289.4 16.2 %collective-permute-start.9 = (bf16[1024,128]{1,0:T(8,128)(2,1)S(1)}, bf16[1024,128]{1,0:T(8,128)(2,1)S(1)}, u32[]{:S(2)}, u32[]{:S(2)}) collective-permute-start(bf16[1024,128]{1,0:T(8,128)(2,1)S(1)} %collective-permute-done.8), channel_id=1, source_target_pairs={{192,0},{0,64},{64,128},{193,1},{1,65},{65,129},{194,2},{2,66},{66... | collective-permute-start | bytes 786440 | tf_op jit(solution)/shard_map/ppermute | solution.py:222
  295.1 13.0 %collective-permute-start.6 = (bf16[1024,128]{1,0:T(8,128)(2,1)}, bf16[1024,128]{1,0:T(8,128)(2,1)S(1)}, u32[]{:S(2)}, u32[]{:S(2)}) collective-permute-start(bf16[1024,128]{1,0:T(8,128)(2,1)} %collective-permute-done.5), channel_id=1, source_target_pairs={{192,0},{0,64},{64,128},{193,1},{1,65},{65,129},{194,2},{2,66},{66... | collective-permute-start | bytes 786440 | tf_op jit(solution)/shard_map/ppermute | solution.py:222
  314.5 62.6 %all-to-all-start.2 = ((bf16[64,16,1024]{2,1,0:T(8,128)(2,1)}), bf16[64,16,1024]{2,1,0:T(8,128)(2,1)}, u32[]{:S(2)}, u32[]{:S(2)}) async-start(bf16[64,16,1024]{2,1,0:T(8,128)(2,1)} %bitcast.62), calls=%async_computation.2 | async-start | bytes 4194304 | tf_op jit(solution)/shard_map/all_to_all | solution.py:21
  382.4 102.0 %all-to-all-start.5 = ((bf16[64,16,2048]{2,1,0:T(8,128)(2,1)}), bf16[64,16,2048]{2,1,0:T(8,128)(2,1)}, u32[]{:S(2)}, u32[]{:S(2)}) async-start(bf16[64,16,2048]{2,1,0:T(8,128)(2,1)} %bitcast.63), calls=%async_computation.5 | async-start | bytes 8388608 | tf_op jit(solution)/shard_map/all_to_all | solution.py:21
  390.0 25.8 %collective-permute-start.20 = (bf16[1024,512]{1,0:T(8,128)(2,1)S(1)}, bf16[1024,512]{1,0:T(8,128)(2,1)}, u32[]{:S(2)}, u32[]{:S(2)}) collective-permute-start(bf16[1024,512]{1,0:T(8,128)(2,1)S(1)} %pad_maximum_fusion), channel_id=1, source_target_pairs={{0,128},{1,129},{2,130},{3,131},{4,132},{5,133},{6,134},{7,135},{8... | collective-permute-start | bytes 3145736 | tf_op jit(solution)/shard_map/ppermute | solution.py:250
  394.9 43.5 %collective-permute-start.21 = (bf16[1024,512]{1,0:T(8,128)(2,1)}, bf16[1024,512]{1,0:T(8,128)(2,1)}, u32[]{:S(2)}, u32[]{:S(2)}) collective-permute-start(bf16[1024,512]{1,0:T(8,128)(2,1)} %add_convert_fusion.1), channel_id=1, source_target_pairs={{0,64},{1,65},{2,66},{3,67},{4,68},{5,69},{6,70},{7,71},{8,72},{9,... | collective-permute-start | bytes 3145736 | tf_op jit(solution)/shard_map/ppermute | solution.py:250
  397.2 41.2 %collective-permute-start.19 = (bf16[1024,512]{1,0:T(8,128)(2,1)}, bf16[1024,512]{1,0:T(8,128)(2,1)}, u32[]{:S(2)}, u32[]{:S(2)}) collective-permute-start(bf16[1024,512]{1,0:T(8,128)(2,1)} %add_convert_fusion.2), channel_id=1, source_target_pairs={{0,192},{1,193},{2,194},{3,195},{4,196},{5,197},{6,198},{7,199},{8... | collective-permute-start | bytes 3145736 | tf_op jit(solution)/shard_map/ppermute | solution.py:250
  (51 other events, 532.8 us)

commit v4 on v2

--- a/solution.py
+++ b/solution.py
@@ -20,6 +20,13 @@
     blocks = rows.reshape(devices, tile, rows.shape[1])
     blocks = lax.all_to_all(blocks, "seq", split_axis=0, concat_axis=0)
     return blocks.reshape(rows.shape)
+
+
+def sent_to_natural(count, order):
+    chunk, tile = order // count, count * count
+    m = lax.broadcasted_iota(jnp.int32, (order, order), 0)
+    n = lax.broadcasted_iota(jnp.int32, (order, order), 1)
+    return (m == (n // count % count) * chunk + (n // tile) * count + n % count).astype(BF16)
 
 
 def reorder_kernel(count, gain, rows_in, rows_out):
@@ -58,6 +65,59 @@
     )(*operands)
 
 
+def restore_kernel(count, rows_in, rows_out):
+    placed = dot(sent_to_natural(count, rows_in.shape[0]), rows_in[...]).astype(BF16)
+    rows_out[...] = placed.reshape(rows_out.shape)
+
+
+def restore(rows_in, count):
+    rows, channels = rows_in.shape
+    order = rows // count
+    return pl.pallas_call(
+        functools.partial(restore_kernel, count),
+        out_shape=jax.ShapeDtypeStruct((count, order, channels), BF16),
+        grid=(count,),
+        in_specs=[pl.BlockSpec((order, channels), lambda n: (n, 0))],
+        out_specs=pl.BlockSpec((count, order // count, channels), lambda n: (0, n, 0)),
+        cost_estimate=pl.CostEstimate(
+            flops=2 * rows * order * channels, bytes_accessed=4 * rows * channels, transcendentals=0
+        ),
+    )(rows_in).reshape(rows_in.shape)
+
+
+def final_kernel(count, factors, columns, source, gain, result):
+    order = factors.shape[1]
+    chunk = order // count
+    place = sent_to_natural(count, order)
+    groups = [dot(place, columns[g * order:(g + 1) * order, :]).astype(BF16) for g in range(count)]
+    for il in range(count):
+        mine = jnp.concatenate([g[il * chunk:(il + 1) * chunk, :] for g in groups], axis=0)
+        spread = dot(factors[il], mine)
+        part = slice(il * order, (il + 1) * order)
+        result[part, :] = (source[part, :].astype(F32) + gain[...] * spread).astype(BF16)
+
+
+def final_product(factors, columns, source, gain, width=512):
+    count, order = factors.shape[:2]
+    rows, channels = columns.shape
+    block = pl.BlockSpec((rows, width), lambda n: (0, n))
+    return pl.pallas_call(
+        functools.partial(final_kernel, count),
+        out_shape=jax.ShapeDtypeStruct((rows, channels), BF16),
+        grid=(channels // width,),
+        in_specs=[
+            pl.BlockSpec(factors.shape, lambda n: (0, 0, 0), pipeline_mode=pl.Buffered(1)),
+            block,
+            block,
+            pl.BlockSpec((1, width), lambda n: (0, n)),
+        ],
+        out_specs=block,
+        cost_estimate=pl.CostEstimate(
+            flops=4 * rows * order * channels, bytes_accessed=6 * rows * channels, transcendentals=0
+        ),
+    )(factors, columns, source, gain)
+
+
 def scale_kernel(flag, gain, here, moved, *rest):
     gradient = jnp.where(flag[0] == 1, here[...].astype(F32), moved[...].astype(F32))
     rest[-1][...] = (gradient * gain[...].astype(F32)).astype(BF16)
@@ -65,11 +125,12 @@
 
 def scale_into(flag, gain, here, moved, total, at, buffer=None):
     rows, width = here.shape
-    step, column = rows // 2, at // width
-    block = pl.BlockSpec((step, width), lambda n: (n, 0))
+    unit = min(256, width)
+    step, column = rows // 2, at // unit
+    block = pl.BlockSpec((step, unit), lambda n, m: (n, m))
     in_specs = [
         pl.BlockSpec(memory_space=pltpu.SMEM),
-        pl.BlockSpec((1, width), lambda n: (0, 0)),
+        pl.BlockSpec((1, unit), lambda n, m: (0, m)),
         block,
         block,
     ]
@@ -82,9 +143,9 @@
     return pl.pallas_call(
         scale_kernel,
         out_shape=jax.ShapeDtypeStruct((rows, total), BF16),
-        grid=(2,),
+        grid=(2, width // unit),
         in_specs=in_specs,
-        out_specs=pl.BlockSpec((step, width), lambda n: (n, column)),
+        out_specs=pl.BlockSpec((step, unit), lambda n, m: (n, column + m)),
         input_output_aliases=aliases,
         cost_estimate=pl.CostEstimate(flops=rows * width, bytes_accessed=6 * rows * width, transcendentals=0),
     )(*operands)
@@ -136,7 +197,6 @@
 
     out = lax.broadcasted_iota(jnp.int32, (rows, rows), 0)
     into = lax.broadcasted_iota(jnp.int32, (rows, rows), 1)
-    natural = (out // count % count) * order + (out // tile) * count + out % count
 
     at = lax.broadcasted_iota(jnp.int32, (count, rows, order), 1)
     col = lax.broadcasted_iota(jnp.int32, (count, rows, order), 2)
@@ -153,7 +213,6 @@
     first_spread = jnp.where(out // order == into // count % count, wide, 0.0).astype(BF16)
 
     inner, outer = inner_gain, outer_gain.astype(F32)
-    restore = (natural.T == into.T).astype(BF16)
     first_sent = reorder(first_spread, count)
 
     def mix(columns):
@@ -163,7 +222,6 @@
         spread = dot(weights, returned)
         return (gradient.astype(F32) + outer[:, cols] * spread).astype(BF16)
 
-    whole = slice(0, channels)
     halves = (slice(0, channels // 2), slice(channels // 2, channels))
     per_half = sections // 2
 
@@ -172,38 +230,31 @@
     reordered = reorder(arriving[0], count)
     loss_sent = reorder(loss_grad, count)
     lost = [loss_sent if q == last else lax.ppermute(loss_sent, "pipe", [(q, last)]) for q in range(sections)]
-    around = piece // sections
-    cuts = ((0, piece - around, False), (piece - around, around, True), (piece, piece, False))
-    here = [
-        [lost[n * per_half + start // piece][:, start % piece:start % piece + width] for start, width, _ in cuts]
-        for n in range(2)
-    ]
-    columns, here, first_sent, reordered = lax.optimization_barrier((first_sending, here, first_sent, reordered))
+    cuts = ((0, piece // 2), (piece // 2, piece), (piece // 2 + piece, piece // 2))
+    here = []
+    for n in range(2):
+        both = jnp.concatenate(lost[n * per_half:(n + 1) * per_half], axis=1)
+        here.append([both[:, start:start + width] for start, width in cuts])
+    turned = jnp.swapaxes(first, 1, 2)
+    columns, here, first_sent, reordered, turned = lax.optimization_barrier(
+        (first_sending, here, first_sent, reordered, turned)
+    )
 
     back = [(i + 1, i) for i in range(sections - 1)]
     returned = [exchange(mix(columns[:, h]), devices) for h in halves]
     flag = (position == last).astype(jnp.int32).reshape(1)
 
-    def shift(block, round_about):
-        if not round_about:
-            return lax.ppermute(block, "pipe", back)
-        for hop in range(last):
-            route = [((i + 1 + hop) % sections, (i + 2 + hop) % sections) for i in range(last)]
-            block = lax.ppermute(block, "pipe", route)
-        return block
-
     def step(n):
         passed, moved = [], []
-        for c, (start, width, round_about) in enumerate(cuts):
+        for c, (start, width) in enumerate(cuts):
             cols = slice(halves[n].start + start, halves[n].start + start + width)
             passed.append(finish(reordered[:, cols], first_sent, returned[n][:, start:start + width], cols))
-            moved.append(shift(passed[c], round_about))
+            moved.append(lax.ppermute(passed[c], "pipe", back))
         return passed, moved
 
     def fill(n, moved):
         buffer = None
-        for c in (1, 2, 0):
-            start, width, _ = cuts[c]
+        for c, (start, width) in enumerate(cuts):
             gain = inner[:, halves[n].start + start:halves[n].start + start + width]
             buffer = scale_into(flag, gain, here[n][c], moved[c], channels // 2, start, buffer)
         return buffer
@@ -212,23 +263,23 @@
     for n in range(2):
         done, shifted = step(n)
         sent.append(exchange(fill(n, shifted), devices))
-        passed.append(done)
+        passed.append(jnp.concatenate(done, axis=1))
         moved += shifted
 
-    leaving = jnp.concatenate(passed[0][:2], axis=1)
+    leaving = passed[0][:, :piece]
     for q in range(1, sections):
-        parts = passed[q // per_half][:2] if q % per_half == 0 else passed[q // per_half][2:]
-        parts = jnp.concatenate([lax.ppermute(p, "pipe", [(0, q)]) for p in parts], axis=1)
-        leaving = jnp.where(position == q, parts, leaving)
-    leaving = dot(restore, leaving).astype(BF16)
+        start = q % per_half * piece
+        part = lax.ppermute(passed[q // per_half][:, start:start + piece], "pipe", [(0, q)])
+        leaving = jnp.where(position == q, part, leaving)
+    leaving = restore(leaving, count)
 
     mixed = product_into(second_spread, sent[0], channels, 0)
     mixed = product_into(second_spread, sent[1], channels, channels // 2, mixed)
     final = exchange(mixed, devices)
     source = jnp.concatenate([jnp.where(position == last, a, b) for a, b in zip(here[0] + here[1], moved)], axis=1)
-    source = dot(restore, source).astype(BF16)
+    source = restore(source, count)
     final, source, leaving = lax.optimization_barrier((final, source, leaving))
-    entering = finish(source, first_spread, final, whole)
+    entering = final_product(turned, final, source, outer)
     return entering[None], leaving
 
 

time: 486 us -> 487 us (level)
  Pallas kernels: 39.4 us -> 59.1 us
  matrix products: 49.8 us -> 31.8 us
  other arithmetic: 7.45 us -> 22.9 us
  starting transfers between devices: 94.4 us -> 80.3 us
    all_to_all x6, waiting for transfers between devices: 168 us -> 150 us  [exchange(): blocks = lax.all_to_all(blocks, 'seq', split_axis=0, concat_axis=0)]
    dot_general x12 -> x9, matrix products: 49 us -> 31 us  [dot(): lax.dot_general(a, b, (((1,), (0,)), ((), ())), preferred_element_type=F32)]
    pallas_call x0 -> x3, Pallas kernels: none -> 17.3 us  [the longest x2 9.47 us: restore(): pl.pallas_call(functools.partial(restore_kernel, count), out_shape=jax.Sh...]
    ppermute x14 -> x9, waiting for transfers between devices: 84.5 us -> 101 us  [the longest x6 64.1 us: step(): moved.append(lax.ppermute(passed[c], 'pipe', back))]
    ppermute x14 -> x9, starting transfers between devices: 32 us -> 17 us  [the longest x3 9.34 us: local_program(): lax.ppermute(passed[q // per_half][:, start:start + piece], 'pipe', [(0,...]
    concatenate x0 -> x4, other arithmetic: none -> 9.39 us  [the longest x2 4.99 us: local_program(): passed.append(jnp.concatenate(done, axis=1))]
  transfers between devices with their start and end apart: 23 -> 18, of which waited for: 13 -> 12; matrix products, arithmetic and copies ran while one was open for 11% -> 12% of each run, Pallas kernels for 6% -> 9%
where the time goes in v4:
time: 487 us; the launch traced here: 485 us
  waiting for transfers between devices  275 us (56%)
  starting transfers between devices  80.3 us (16%)
  Pallas kernels  59.1 us (12%)
  matrix products  31.8 us (7%)
  other arithmetic  22.9 us (5%)
  local copies, waits for them, and re-layouts  14.4 us (3%)
    all_to_all x6, waiting for transfers between devices, exchange(): blocks = lax.all_to_all(blocks, 'seq', split_axis=0, concat_axis=0)  150 us
    ppermute x6, waiting for transfers between devices, step(): moved.append(lax.ppermute(passed[c], 'pipe', back))  64.1 us
    all_to_all x6, starting transfers between devices, exchange(): blocks = lax.all_to_all(blocks, 'seq', split_axis=0, concat_axis=0)  54.6 us
    ppermute x3, waiting for transfers between devices, local_program(): lax.ppermute(passed[q // per_half][:, start:start + piece], 'pipe', [(0,...  36.5 us
    dot_general x9, matrix products, dot(): lax.dot_general(a, b, (((1,), (0,)), ((), ())), preferred_element_type=F32)  31 us
    ppermute x3, waiting for transfers between devices, local_program(): lax.ppermute(loss_sent, 'pipe', [(q, last)])  24.9 us
    pallas_call x6, Pallas kernels, scale_into(): pl.pallas_call(scale_kernel, out_shape=jax.ShapeDtypeStruct((rows, total)...  15.5 us
    pallas_call x4, Pallas kernels, reorder(): pl.pallas_call(kernel, out_shape=jax.ShapeDtypeStruct(rows_in.shape, BF16...  15.5 us
  transfers between devices with their start and end apart: 18, of which 12 were waited for; matrix products, arithmetic and copies ran while one was open for 12% of the time, Pallas kernels for 9%

profile of v4, /device:TPU:1, one launch (start us, length us, event | category | flops | bytes accessed | tf_op | source)
XLA Modules:
  0.0 484.8 jit_solution(1324155907135798775)
XLA Ops:
  5.3 13.3 %all-to-all-start = ((bf16[64,16,2048]{2,1,0:T(8,128)(2,1)}), bf16[64,16,2048]{2,1,0:T(8,128)(2,1)}, u32[]{:S(2)}, u32[]{:S(2)}) async-start(bf16[64,16,2048]{2,1,0:T(8,128)(2,1)} %bitcast.61), calls=%async_computation | async-start | bytes 8388608 | tf_op jit(solution)/shard_map/all_to_all | solution.py:21
  21.3 5.4 %collective-permute-start = (bf16[1024,512]{1,0:T(8,128)(2,1)}, bf16[1024,512]{1,0:T(8,128)(2,1)}, u32[]{:S(2)}, u32[]{:S(2)}) collective-permute-start(bf16[1024,512]{1,0:T(8,128)(2,1)} %shard_map.78), channel_id=1, source_target_pairs={{0,192},{1,193},{2,194},{3,195},{4,196},{5,197},{6,198},{7,199},{8... | collective-permute-start | bytes 3145736 | tf_op jit(solution)/shard_map/ppermute | solution.py:232
  45.5 24.9 %collective-permute-done = bf16[1024,512]{1,0:T(8,128)(2,1)} collective-permute-done((bf16[1024,512]{1,0:T(8,128)(2,1)}, bf16[1024,512]{1,0:T(8,128)(2,1)}, u32[]{:S(2)}, u32[]{:S(2)}) %collective-permute-start) | collective-permute-done | bytes 1048608 | tf_op jit(solution)/shard_map/ppermute | solution.py:232
  80.6 33.9 %all-to-all-done = bf16[64,16,2048]{2,1,0:T(8,128)(2,1)} async-done(((bf16[64,16,2048]{2,1,0:T(8,128)(2,1)}), bf16[64,16,2048]{2,1,0:T(8,128)(2,1)}, u32[]{:S(2)}, u32[]{:S(2)}) %all-to-all-start) | async-done | bytes 4194336 | tf_op jit(solution)/shard_map/all_to_all | solution.py:21
  114.5 5.2 %fusion.12 = bf16[1024,1024]{1,0:T(8,128)(2,1)} fusion(bf16[1024,1024]{1,0:T(8,128)(2,1)S(1)} %select_convert_fusion.weights, bf16[1024,2048]{1,0:T(8,128)(2,1)} %bitcast.2), kind=kOutput, calls=%fused_computation.21 | convolution fusion | flops 2148532224 | bytes 6291456 | tf_op jit(solution)/shard_map/dot_general | solution.py:15
  119.7 5.9 %all-to-all-start.3 = ((bf16[64,16,1024]{2,1,0:T(8,128)(2,1)}), bf16[64,16,1024]{2,1,0:T(8,128)(2,1)}, u32[]{:S(2)}, u32[]{:S(2)}) async-start(bf16[64,16,1024]{2,1,0:T(8,128)(2,1)} %bitcast.67), calls=%async_computation.3 | async-start | bytes 4194304 | tf_op jit(solution)/shard_map/all_to_all | solution.py:21
  125.6 5.2 %fusion.9 = bf16[1024,1024]{1,0:T(8,128)(2,1)} fusion(bf16[1024,1024]{1,0:T(8,128)(2,1)S(1)} %select_convert_fusion.weights, bf16[1024,2048]{1,0:T(8,128)(2,1)} %bitcast.2), kind=kOutput, calls=%fused_computation.20 | convolution fusion | flops 2148532224 | bytes 6291456 | tf_op jit(solution)/shard_map/dot_general | solution.py:15
  130.9 45.9 %all-to-all-done.3 = bf16[64,16,1024]{2,1,0:T(8,128)(2,1)} async-done(((bf16[64,16,1024]{2,1,0:T(8,128)(2,1)}), bf16[64,16,1024]{2,1,0:T(8,128)(2,1)}, u32[]{:S(2)}, u32[]{:S(2)}) %all-to-all-start.3) | async-done | bytes 2097184 | tf_op jit(solution)/shard_map/all_to_all | solution.py:21
  176.7 6.2 %all-to-all-start.1 = ((bf16[64,16,1024]{2,1,0:T(8,128)(2,1)}), bf16[64,16,1024]{2,1,0:T(8,128)(2,1)}, u32[]{:S(2)}, u32[]{:S(2)}) async-start(bf16[64,16,1024]{2,1,0:T(8,128)(2,1)} %bitcast.66), calls=%async_computation.1 | async-start | bytes 4194304 | tf_op jit(solution)/shard_map/all_to_all | solution.py:21
  197.1 26.8 %collective-permute-done.8.moved = bf16[1024,256]{1,0:T(8,128)(2,1)S(1)} collective-permute-done((bf16[1024,256]{1,0:T(8,128)(2,1)}, bf16[1024,256]{1,0:T(8,128)(2,1)S(1)}, u32[]{:S(2)}, u32[]{:S(2)}) %collective-permute-start.8) | collective-permute-done | bytes 524320 | tf_op jit(solution)/shard_map/ppermute | solution.py:252
  237.9 11.3 %all-to-all-start.4 = ((bf16[64,16,1024]{2,1,0:T(8,128)(2,1)}), bf16[64,16,1024]{2,1,0:T(8,128)(2,1)S(1)}, u32[]{:S(2)}, u32[]{:S(2)}) async-start(bf16[64,16,1024]{2,1,0:T(8,128)(2,1)} %bitcast.58), calls=%async_computation.4 | async-start | bytes 4194304 | tf_op jit(solution)/shard_map/all_to_all | solution.py:21
  262.4 29.0 %collective-permute-done.5.moved = bf16[1024,256]{1,0:T(8,128)(2,1)S(1)} collective-permute-done((bf16[1024,256]{1,0:T(8,128)(2,1)S(1)}, bf16[1024,256]{1,0:T(8,128)(2,1)S(1)}, u32[]{:S(2)}, u32[]{:S(2)}) %collective-permute-start.5) | collective-permute-done | bytes 524320 | tf_op jit(solution)/shard_map/ppermute | solution.py:252
  297.9 4.7 collective-permute-done.3.moved
  306.8 11.4 %all-to-all-start.2 = ((bf16[64,16,1024]{2,1,0:T(8,128)(2,1)}), bf16[64,16,1024]{2,1,0:T(8,128)(2,1)}, u32[]{:S(2)}, u32[]{:S(2)}) async-start(bf16[64,16,1024]{2,1,0:T(8,128)(2,1)} %bitcast.57), calls=%async_computation.2 | async-start | bytes 4194304 | tf_op jit(solution)/shard_map/all_to_all | solution.py:21
  318.2 5.4 %shard_map.87.rest_0_ = bf16[1024,2048]{1,0:T(8,128)(2,1)} custom-call(bf16[1024,1024]{1,0:T(8,128)(2,1)} %copy-done.5, bf16[1024,1024]{1,0:T(8,128)(2,1)} %bitcast.63), custom_call_target="tpu_custom_call" | custom-call | flops 2147483648 | bytes 6291456 | tf_op jit(solution)/shard_map/pallas_call | solution.py:172
  323.7 45.7 %all-to-all-done.2 = bf16[64,16,1024]{2,1,0:T(8,128)(2,1)} async-done(((bf16[64,16,1024]{2,1,0:T(8,128)(2,1)}), bf16[64,16,1024]{2,1,0:T(8,128)(2,1)}, u32[]{:S(2)}, u32[]{:S(2)}) %all-to-all-start.2) | async-done | bytes 2097184 | tf_op jit(solution)/shard_map/all_to_all | solution.py:21
  369.4 5.4 %shard_map.88 = bf16[1024,2048]{1,0:T(8,128)(2,1)} custom-call(bf16[1024,1024]{1,0:T(8,128)(2,1)} %copy-done.5, bf16[1024,1024]{1,0:T(8,128)(2,1)} %bitcast.17.columns, bf16[1024,2048]{1,0:T(8,128)(2,1)} %shard_map.87.rest_0_), custom_call_target="tpu_custom_call", output_to_operand_aliasing={{}: (2, {})} | custom-call | flops 2147483648 | bytes 6291456 | tf_op jit(solution)/shard_map/pallas_call | solution.py:172
  374.8 6.4 %all-to-all-start.5 = ((bf16[64,16,2048]{2,1,0:T(8,128)(2,1)}), bf16[64,16,2048]{2,1,0:T(8,128)(2,1)}, u32[]{:S(2)}, u32[]{:S(2)}) async-start(bf16[64,16,2048]{2,1,0:T(8,128)(2,1)} %bitcast.56), calls=%async_computation.5 | async-start | bytes 8388608 | tf_op jit(solution)/shard_map/all_to_all | solution.py:21
  384.1 4.8 collective-permute-start.10
  397.1 14.0 %collective-permute-done.10 = bf16[1024,512]{1,0:T(8,128)(2,1)S(1)} collective-permute-done((bf16[1024,512]{1,0:T(8,128)(2,1)}, bf16[1024,512]{1,0:T(8,128)(2,1)S(1)}, u32[]{:S(2)}, u32[]{:S(2)}) %collective-permute-start.10) | collective-permute-done | bytes 1048608 | tf_op jit(solution)/shard_map/ppermute | solution.py:272
  414.5 19.0 %collective-permute-done.11 = bf16[1024,512]{1,0:T(8,128)(2,1)} collective-permute-done((bf16[1024,512]{1,0:T(8,128)(2,1)}, bf16[1024,512]{1,0:T(8,128)(2,1)}, u32[]{:S(2)}, u32[]{:S(2)}) %collective-permute-start.11) | collective-permute-done | bytes 1048608 | tf_op jit(solution)/shard_map/ppermute | solution.py:272
  447.0 5.5 %shard_map.89 = bf16[4,256,2048]{2,1,0:T(8,128)(2,1)} custom-call(bf16[1024,2048]{1,0:T(8,128)(2,1)} %select_dynamic-update-slice_fusion.2.rows_in), custom_call_target="tpu_custom_call" | custom-call | flops 1073741824 | bytes 8388608 | tf_op jit(solution)/shard_map/pallas_call | solution.py:76
  452.5 24.5 %all-to-all-done.5 = bf16[64,16,2048]{2,1,0:T(8,128)(2,1)} async-done(((bf16[64,16,2048]{2,1,0:T(8,128)(2,1)}), bf16[64,16,2048]{2,1,0:T(8,128)(2,1)}, u32[]{:S(2)}, u32[]{:S(2)}) %all-to-all-start.5) | async-done | bytes 4194336 | tf_op jit(solution)/shard_map/all_to_all | solution.py:21
  477.0 7.8 %shard_map.91 = bf16[1024,2048]{1,0:T(8,128)(2,1)} custom-call(bf16[4,256,256]{2,1,0:T(8,128)(2,1)} %bitcast.65, bf16[1024,2048]{1,0:T(8,128)(2,1)} %bitcast.26.columns, bf16[1024,2048]{1,0:T(8,128)(2,1)} %bitcast.62, f32[1,2048]{1,0:T(1,128)} %convert_element_type.62.gain), custom_call_target="tpu_custom_call" | custom-call | flops 2147483648 | bytes 12582912 | tf_op jit(solution)/shard_map/pallas_call | solution.py:104
  (128 shorter events, 116.0 us)
Async XLA Ops:
  0.6 42.7 %copy-start = (bf16[1,4,256,256]{3,2,1,0:T(8,128)(2,1)S(1)}, bf16[1,4,256,256]{3,2,1,0:T(8,128)(2,1)}, u32[]{:S(2)}) copy-start(bf16[1,4,256,256]{3,2,1,0:T(8,128)(2,1)} %param.9) | copy-start | bytes 1572868
  5.3 109.2 %all-to-all-start = ((bf16[64,16,2048]{2,1,0:T(8,128)(2,1)}), bf16[64,16,2048]{2,1,0:T(8,128)(2,1)}, u32[]{:S(2)}, u32[]{:S(2)}) async-start(bf16[64,16,2048]{2,1,0:T(8,128)(2,1)} %bitcast.61), calls=%async_computation | async-start | bytes 8388608 | tf_op jit(solution)/shard_map/all_to_all | solution.py:21
  18.6 11.4 %copy-start.26 = (bf16[1,4,256,256]{3,2,1,0:T(8,128)(2,1)S(1)}, bf16[1,4,256,256]{3,2,1,0:T(8,128)(2,1)}, u32[]{:S(2)}) copy-start(bf16[1,4,256,256]{3,2,1,0:T(8,128)(2,1)} %param.8) | copy-start | bytes 1572868
  21.3 49.1 %collective-permute-start = (bf16[1024,512]{1,0:T(8,128)(2,1)}, bf16[1024,512]{1,0:T(8,128)(2,1)}, u32[]{:S(2)}, u32[]{:S(2)}) collective-permute-start(bf16[1024,512]{1,0:T(8,128)(2,1)} %shard_map.78), channel_id=1, source_target_pairs={{0,192},{1,193},{2,194},{3,195},{4,196},{5,197},{6,198},{7,199},{8... | collective-permute-start | bytes 3145736 | tf_op jit(solution)/shard_map/ppermute | solution.py:232
  26.7 45.7 %collective-permute-start.1 = (bf16[1024,512]{1,0:T(8,128)(2,1)}, bf16[1024,512]{1,0:T(8,128)(2,1)}, u32[]{:S(2)}, u32[]{:S(2)}) collective-permute-start(bf16[1024,512]{1,0:T(8,128)(2,1)} %shard_map.78), channel_id=1, source_target_pairs={{64,192},{65,193},{66,194},{67,195},{68,196},{69,197},{70,198},{71... | collective-permute-start | bytes 3145736 | tf_op jit(solution)/shard_map/ppermute | solution.py:232
  28.3 45.9 %collective-permute-start.2 = (bf16[1024,512]{1,0:T(8,128)(2,1)}, bf16[1024,512]{1,0:T(8,128)(2,1)}, u32[]{:S(2)}, u32[]{:S(2)}) collective-permute-start(bf16[1024,512]{1,0:T(8,128)(2,1)} %shard_map.78), channel_id=1, source_target_pairs={{128,192},{129,193},{130,194},{131,195},{132,196},{133,197},{134,1... | collective-permute-start | bytes 3145736 | tf_op jit(solution)/shard_map/ppermute | solution.py:232
  45.5 80.1 %copy-start.5 = (bf16[1024,1024]{1,0:T(8,128)(2,1)}, bf16[1024,1024]{1,0:T(8,128)(2,1)S(1)}, u32[]{:S(2)}) copy-start(bf16[1024,1024]{1,0:T(8,128)(2,1)S(1)} %select_convert_fusion.weights) | copy-start | bytes 6291460
  119.7 57.1 %all-to-all-start.3 = ((bf16[64,16,1024]{2,1,0:T(8,128)(2,1)}), bf16[64,16,1024]{2,1,0:T(8,128)(2,1)}, u32[]{:S(2)}, u32[]{:S(2)}) async-start(bf16[64,16,1024]{2,1,0:T(8,128)(2,1)} %bitcast.67), calls=%async_computation.3 | async-start | bytes 4194304 | tf_op jit(solution)/shard_map/all_to_all | solution.py:21
  176.7 61.1 %all-to-all-start.1 = ((bf16[64,16,1024]{2,1,0:T(8,128)(2,1)}), bf16[64,16,1024]{2,1,0:T(8,128)(2,1)}, u32[]{:S(2)}, u32[]{:S(2)}) async-start(bf16[64,16,1024]{2,1,0:T(8,128)(2,1)} %bitcast.66), calls=%async_computation.1 | async-start | bytes 4194304 | tf_op jit(solution)/shard_map/all_to_all | solution.py:21
  186.5 40.2 %collective-permute-start.7 = (bf16[1024,512]{1,0:T(8,128)(2,1)S(1)}, bf16[1024,512]{1,0:T(8,128)(2,1)S(1)}, u32[]{:S(2)}, u32[]{:S(2)}) collective-permute-start(bf16[1024,512]{1,0:T(8,128)(2,1)S(1)} %add_convert_fusion), channel_id=1, source_target_pairs={{64,0},{128,64},{192,128},{65,1},{129,65},{193,129},{66,2},{130,66... | collective-permute-start | bytes 3145736 | tf_op jit(solution)/shard_map/ppermute | solution.py:252
  190.6 33.4 %collective-permute-start.8 = (bf16[1024,256]{1,0:T(8,128)(2,1)}, bf16[1024,256]{1,0:T(8,128)(2,1)S(1)}, u32[]{:S(2)}, u32[]{:S(2)}) collective-permute-start(bf16[1024,256]{1,0:T(8,128)(2,1)} %fusion.23), channel_id=1, source_target_pairs={{64,0},{128,64},{192,128},{65,1},{129,65},{193,129},{66,2},{130,66... | collective-permute-start | bytes 1572872 | tf_op jit(solution)/shard_map/ppermute | solution.py:252
  194.7 40.4 %collective-permute-start.6 = (bf16[1024,256]{1,0:T(8,128)(2,1)}, bf16[1024,256]{1,0:T(8,128)(2,1)S(1)}, u32[]{:S(2)}, u32[]{:S(2)}) collective-permute-start(bf16[1024,256]{1,0:T(8,128)(2,1)} %fusion.22), channel_id=1, source_target_pairs={{64,0},{128,64},{192,128},{65,1},{129,65},{193,129},{66,2},{130,66... | collective-permute-start | bytes 1572872 | tf_op jit(solution)/shard_map/ppermute | solution.py:252
  237.9 67.5 %all-to-all-start.4 = ((bf16[64,16,1024]{2,1,0:T(8,128)(2,1)}), bf16[64,16,1024]{2,1,0:T(8,128)(2,1)S(1)}, u32[]{:S(2)}, u32[]{:S(2)}) async-start(bf16[64,16,1024]{2,1,0:T(8,128)(2,1)} %bitcast.58), calls=%async_computation.4 | async-start | bytes 4194304 | tf_op jit(solution)/shard_map/all_to_all | solution.py:21
  253.8 40.4 %collective-permute-start.4 = (bf16[1024,512]{1,0:T(8,128)(2,1)}, bf16[1024,512]{1,0:T(8,128)(2,1)}, u32[]{:S(2)}, u32[]{:S(2)}) collective-permute-start(bf16[1024,512]{1,0:T(8,128)(2,1)} %add_convert_fusion.1), channel_id=1, source_target_pairs={{64,0},{128,64},{192,128},{65,1},{129,65},{193,129},{66,2},{130,66... | collective-permute-start | bytes 3145736 | tf_op jit(solution)/shard_map/ppermute | solution.py:252
  257.0 34.3 %collective-permute-start.5 = (bf16[1024,256]{1,0:T(8,128)(2,1)S(1)}, bf16[1024,256]{1,0:T(8,128)(2,1)S(1)}, u32[]{:S(2)}, u32[]{:S(2)}) collective-permute-start(bf16[1024,256]{1,0:T(8,128)(2,1)S(1)} %fusion.21), channel_id=1, source_target_pairs={{64,0},{128,64},{192,128},{65,1},{129,65},{193,129},{66,2},{130,66... | collective-permute-start | bytes 1572872 | tf_op jit(solution)/shard_map/ppermute | solution.py:252
  261.1 41.5 %collective-permute-start.3 = (bf16[1024,256]{1,0:T(8,128)(2,1)}, bf16[1024,256]{1,0:T(8,128)(2,1)S(1)}, u32[]{:S(2)}, u32[]{:S(2)}) collective-permute-start(bf16[1024,256]{1,0:T(8,128)(2,1)} %fusion.20), channel_id=1, source_target_pairs={{64,0},{128,64},{192,128},{65,1},{129,65},{193,129},{66,2},{130,66... | collective-permute-start | bytes 1572872 | tf_op jit(solution)/shard_map/ppermute | solution.py:252
  306.8 62.6 %all-to-all-start.2 = ((bf16[64,16,1024]{2,1,0:T(8,128)(2,1)}), bf16[64,16,1024]{2,1,0:T(8,128)(2,1)}, u32[]{:S(2)}, u32[]{:S(2)}) async-start(bf16[64,16,1024]{2,1,0:T(8,128)(2,1)} %bitcast.57), calls=%async_computation.2 | async-start | bytes 4194304 | tf_op jit(solution)/shard_map/all_to_all | solution.py:21
  374.8 102.2 %all-to-all-start.5 = ((bf16[64,16,2048]{2,1,0:T(8,128)(2,1)}), bf16[64,16,2048]{2,1,0:T(8,128)(2,1)}, u32[]{:S(2)}, u32[]{:S(2)}) async-start(bf16[64,16,2048]{2,1,0:T(8,128)(2,1)} %bitcast.56), calls=%async_computation.5 | async-start | bytes 8388608 | tf_op jit(solution)/shard_map/all_to_all | solution.py:21
  384.1 12.0 %copy-start.11 = (bf16[1024,256]{1,0:T(8,128)(2,1)S(1)}, bf16[1024,256]{1,0:T(8,128)(2,1)}, u32[]{:S(2)}) copy-start(bf16[1024,256]{1,0:T(8,128)(2,1)} %slice.148.here) | copy-start | bytes 1572868
  384.1 12.0 %copy-start.19 = (bf16[1024,256]{1,0:T(8,128)(2,1)S(1)}, bf16[1024,256]{1,0:T(8,128)(2,1)}, u32[]{:S(2)}) copy-start(bf16[1024,256]{1,0:T(8,128)(2,1)} %copy-done.18) | copy-start | bytes 1572868
  384.1 27.0 %collective-permute-start.10 = (bf16[1024,512]{1,0:T(8,128)(2,1)}, bf16[1024,512]{1,0:T(8,128)(2,1)S(1)}, u32[]{:S(2)}, u32[]{:S(2)}) collective-permute-start(bf16[1024,512]{1,0:T(8,128)(2,1)} %get-tuple-element.28), channel_id=1, source_target_pairs={{0,128},{1,129},{2,130},{3,131},{4,132},{5,133},{6,134},{7,135},{8... | collective-permute-start | bytes 3145736 | tf_op jit(solution)/shard_map/ppermute | solution.py:272
  391.0 23.6 %collective-permute-start.9 = (bf16[1024,512]{1,0:T(8,128)(2,1)}, bf16[1024,512]{1,0:T(8,128)(2,1)}, u32[]{:S(2)}, u32[]{:S(2)}) collective-permute-start(bf16[1024,512]{1,0:T(8,128)(2,1)} %get-tuple-element.29), channel_id=1, source_target_pairs={{0,192},{1,193},{2,194},{3,195},{4,196},{5,197},{6,198},{7,199},{8... | collective-permute-start | bytes 3145736 | tf_op jit(solution)/shard_map/ppermute | solution.py:272
  393.3 40.3 %collective-permute-start.11 = (bf16[1024,512]{1,0:T(8,128)(2,1)}, bf16[1024,512]{1,0:T(8,128)(2,1)}, u32[]{:S(2)}, u32[]{:S(2)}) collective-permute-start(bf16[1024,512]{1,0:T(8,128)(2,1)} %pad_maximum_fusion.1), channel_id=1, source_target_pairs={{0,64},{1,65},{2,66},{3,67},{4,68},{5,69},{6,70},{7,71},{8,72},{9,... | collective-permute-start | bytes 3145736 | tf_op jit(solution)/shard_map/ppermute | solution.py:272
  477.0 7.8 %copy-start.1 = (bf16[1,4,256,256]{3,2,1,0:T(8,128)(2,1)S(1)}, bf16[1,4,256,256]{3,2,1,0:T(8,128)(2,1)}, u32[]{:S(2)}) copy-start(bf16[1,4,256,256]{3,2,1,0:T(8,128)(2,1)} %param.9) | copy-start | bytes 1572868
  (25 other events, 80.0 us)

commit v5 on v4

--- a/solution.py
+++ b/solution.py
@@ -142,12 +142,13 @@
         aliases = {4: 0}
     return pl.pallas_call(
         scale_kernel,
-        out_shape=jax.ShapeDtypeStruct((rows, total), BF16),
+        out_shape=pltpu.HBM((rows, total), BF16),
         grid=(2, width // unit),
         in_specs=in_specs,
         out_specs=pl.BlockSpec((step, unit), lambda n, m: (n, column + m)),
         input_output_aliases=aliases,
         cost_estimate=pl.CostEstimate(flops=rows * width, bytes_accessed=6 * rows * width, transcendentals=0),
+        compiler_params=pltpu.CompilerParams(vmem_limit_bytes=24 * 2**20),
     )(*operands)
 
 
@@ -163,7 +164,7 @@
         pl.BlockSpec((rows, depth), lambda n: (0, 0), pipeline_mode=pl.Buffered(1)),
         pl.BlockSpec((depth, width), lambda n: (0, n)),
     ]
-    operands = [weights, columns]
+    operands = [pltpu.with_memory_space_constraint(weights, pltpu.HBM), columns]
     aliases = {}
     if buffer is not None:
         in_specs.append(pl.BlockSpec(memory_space=pl.ANY))
@@ -171,7 +172,7 @@
         aliases = {2: 0}
     return pl.pallas_call(
         product_kernel,
-        out_shape=jax.ShapeDtypeStruct((rows, total), BF16),
+        out_shape=pltpu.HBM((rows, total), BF16),
         grid=(steps,),
         in_specs=in_specs,
         out_specs=pl.BlockSpec((rows, width), lambda n: (0, first + n)),
@@ -181,6 +182,7 @@
             bytes_accessed=2 * (rows * depth + 2 * rows * columns.shape[1]),
             transcendentals=0,
         ),
+        compiler_params=pltpu.CompilerParams(vmem_limit_bytes=24 * 2**20),
     )(*operands)
 
 

time: 487 us -> 484 us (level)
  local copies, waits for them, and re-layouts: 14.4 us -> 7.97 us
  waiting for transfers between devices: 275 us -> 281 us
    ppermute x6, waiting for transfers between devices: 64.1 us -> 70.5 us  [step(): moved.append(lax.ppermute(passed[c], 'pipe', back))]
  transfers between devices with their start and end apart: 18 -> 18, of which waited for: 12 -> 12; matrix products, arithmetic and copies ran while one was open for 12% -> 12% of each run, Pallas kernels for 9% -> 8%
where the time goes in v5:
time: 484 us; the launch traced here: 482 us
  waiting for transfers between devices  281 us (58%)
  starting transfers between devices  80.1 us (17%)
  Pallas kernels  54.7 us (11%)
  matrix products  33.6 us (7%)
  other arithmetic  23.5 us (5%)
  local copies, waits for them, and re-layouts  7.97 us (2%)
    all_to_all x6, waiting for transfers between devices, exchange(): blocks = lax.all_to_all(blocks, 'seq', split_axis=0, concat_axis=0)  152 us
    ppermute x6, waiting for transfers between devices, step(): moved.append(lax.ppermute(passed[c], 'pipe', back))  70.5 us
    all_to_all x6, starting transfers between devices, exchange(): blocks = lax.all_to_all(blocks, 'seq', split_axis=0, concat_axis=0)  54.5 us
    ppermute x3, waiting for transfers between devices, local_program(): lax.ppermute(passed[q // per_half][:, start:start + piece], 'pipe', [(0,...  34.3 us
    dot_general x9, matrix products, dot(): lax.dot_general(a, b, (((1,), (0,)), ((), ())), preferred_element_type=F32)  32.8 us
    ppermute x3, waiting for transfers between devices, local_program(): lax.ppermute(loss_sent, 'pipe', [(q, last)])  24.3 us
    pallas_call x4, Pallas kernels, reorder(): pl.pallas_call(kernel, out_shape=jax.ShapeDtypeStruct(rows_in.shape, BF16...  15.5 us
    pallas_call x6, Pallas kernels, scale_into(): pl.pallas_call(scale_kernel, out_shape=pltpu.HBM((rows, total), BF16), gr...  11.3 us
  transfers between devices with their start and end apart: 18, of which 12 were waited for; matrix products, arithmetic and copies ran while one was open for 12% of the time, Pallas kernels for 8%

profile of v5, /device:TPU:1, one launch (start us, length us, event | category | flops | bytes accessed | tf_op | source)
XLA Modules:
  0.0 482.0 jit_solution(4561512874304534133)
XLA Ops:
  5.3 13.3 %all-to-all-start = ((bf16[64,16,2048]{2,1,0:T(8,128)(2,1)}), bf16[64,16,2048]{2,1,0:T(8,128)(2,1)}, u32[]{:S(2)}, u32[]{:S(2)}) async-start(bf16[64,16,2048]{2,1,0:T(8,128)(2,1)} %bitcast.61), calls=%async_computation | async-start | bytes 8388608 | tf_op jit(solution)/shard_map/all_to_all | solution.py:21
  46.2 24.3 %collective-permute-done = bf16[1024,512]{1,0:T(8,128)(2,1)S(1)} collective-permute-done((bf16[1024,512]{1,0:T(8,128)(2,1)}, bf16[1024,512]{1,0:T(8,128)(2,1)S(1)}, u32[]{:S(2)}, u32[]{:S(2)}) %collective-permute-start) | collective-permute-done | bytes 1048608 | tf_op jit(solution)/shard_map/ppermute | solution.py:234
  76.8 37.6 %all-to-all-done = bf16[64,16,2048]{2,1,0:T(8,128)(2,1)} async-done(((bf16[64,16,2048]{2,1,0:T(8,128)(2,1)}), bf16[64,16,2048]{2,1,0:T(8,128)(2,1)}, u32[]{:S(2)}, u32[]{:S(2)}) %all-to-all-start) | async-done | bytes 4194336 | tf_op jit(solution)/shard_map/all_to_all | solution.py:21
  114.5 5.9 %fusion.12 = bf16[1024,1024]{1,0:T(8,128)(2,1)} fusion(bf16[1024,1024]{1,0:T(8,128)(2,1)} %select_convert_fusion.weights, bf16[1024,2048]{1,0:T(8,128)(2,1)} %bitcast.2), kind=kOutput, calls=%fused_computation.21 | convolution fusion | flops 2148532224 | bytes 6291456 | tf_op jit(solution)/shard_map/dot_general | solution.py:15
  120.3 5.9 %all-to-all-start.3 = ((bf16[64,16,1024]{2,1,0:T(8,128)(2,1)}), bf16[64,16,1024]{2,1,0:T(8,128)(2,1)}, u32[]{:S(2)}, u32[]{:S(2)}) async-start(bf16[64,16,1024]{2,1,0:T(8,128)(2,1)} %bitcast.66), calls=%async_computation.3 | async-start | bytes 4194304 | tf_op jit(solution)/shard_map/all_to_all | solution.py:21
  126.3 5.9 %fusion.9 = bf16[1024,1024]{1,0:T(8,128)(2,1)} fusion(bf16[1024,1024]{1,0:T(8,128)(2,1)} %select_convert_fusion.weights, bf16[1024,2048]{1,0:T(8,128)(2,1)} %bitcast.2), kind=kOutput, calls=%fused_computation.20 | convolution fusion | flops 2148532224 | bytes 6291456 | tf_op jit(solution)/shard_map/dot_general | solution.py:15
  132.1 45.2 %all-to-all-done.3 = bf16[64,16,1024]{2,1,0:T(8,128)(2,1)} async-done(((bf16[64,16,1024]{2,1,0:T(8,128)(2,1)}), bf16[64,16,1024]{2,1,0:T(8,128)(2,1)}, u32[]{:S(2)}, u32[]{:S(2)}) %all-to-all-start.3) | async-done | bytes 2097184 | tf_op jit(solution)/shard_map/all_to_all | solution.py:21
  177.4 6.2 %all-to-all-start.1 = ((bf16[64,16,1024]{2,1,0:T(8,128)(2,1)}), bf16[64,16,1024]{2,1,0:T(8,128)(2,1)}, u32[]{:S(2)}, u32[]{:S(2)}) async-start(bf16[64,16,1024]{2,1,0:T(8,128)(2,1)} %bitcast.65), calls=%async_computation.1 | async-start | bytes 4194304 | tf_op jit(solution)/shard_map/all_to_all | solution.py:21
  197.6 28.2 %collective-permute-done.8.moved = bf16[1024,256]{1,0:T(8,128)(2,1)} collective-permute-done((bf16[1024,256]{1,0:T(8,128)(2,1)}, bf16[1024,256]{1,0:T(8,128)(2,1)}, u32[]{:S(2)}, u32[]{:S(2)}) %collective-permute-start.8) | collective-permute-done | bytes 524320 | tf_op jit(solution)/shard_map/ppermute | solution.py:254
  232.3 4.7 collective-permute-done.6.moved
  238.8 11.5 %all-to-all-start.4 = ((bf16[64,16,1024]{2,1,0:T(8,128)(2,1)}), bf16[64,16,1024]{2,1,0:T(8,128)(2,1)}, u32[]{:S(2)}, u32[]{:S(2)}) async-start(bf16[64,16,1024]{2,1,0:T(8,128)(2,1)} %bitcast.58), calls=%async_computation.4 | async-start | bytes 4194304 | tf_op jit(solution)/shard_map/all_to_all | solution.py:21
  261.9 29.5 %collective-permute-done.5.moved = bf16[1024,256]{1,0:T(8,128)(2,1)S(1)} collective-permute-done((bf16[1024,256]{1,0:T(8,128)(2,1)S(1)}, bf16[1024,256]{1,0:T(8,128)(2,1)S(1)}, u32[]{:S(2)}, u32[]{:S(2)}) %collective-permute-start.5) | collective-permute-done | bytes 524320 | tf_op jit(solution)/shard_map/ppermute | solution.py:254
  294.4 8.1 %collective-permute-done.3.moved = bf16[1024,256]{1,0:T(8,128)(2,1)S(1)} collective-permute-done((bf16[1024,256]{1,0:T(8,128)(2,1)S(1)}, bf16[1024,256]{1,0:T(8,128)(2,1)S(1)}, u32[]{:S(2)}, u32[]{:S(2)}) %collective-permute-start.3) | collective-permute-done | bytes 524320 | tf_op jit(solution)/shard_map/ppermute | solution.py:254
  304.2 11.5 %all-to-all-start.2 = ((bf16[64,16,1024]{2,1,0:T(8,128)(2,1)}), bf16[64,16,1024]{2,1,0:T(8,128)(2,1)}, u32[]{:S(2)}, u32[]{:S(2)}) async-start(bf16[64,16,1024]{2,1,0:T(8,128)(2,1)} %bitcast.57), calls=%async_computation.2 | async-start | bytes 4194304 | tf_op jit(solution)/shard_map/all_to_all | solution.py:21
  315.8 5.4 %shard_map.87.rest_0_ = bf16[1024,2048]{1,0:T(8,128)(2,1)} custom-call(bf16[1024,1024]{1,0:T(8,128)(2,1)} %select_convert_fusion.weights, bf16[1024,1024]{1,0:T(8,128)(2,1)} %bitcast.24.columns), custom_call_target="tpu_custom_call" | custom-call | flops 2147483648 | bytes 6291456 | tf_op jit(solution)/shard_map/pallas_call | solution.py:173
  321.2 45.7 %all-to-all-done.2 = bf16[64,16,1024]{2,1,0:T(8,128)(2,1)} async-done(((bf16[64,16,1024]{2,1,0:T(8,128)(2,1)}), bf16[64,16,1024]{2,1,0:T(8,128)(2,1)}, u32[]{:S(2)}, u32[]{:S(2)}) %all-to-all-start.2) | async-done | bytes 2097184 | tf_op jit(solution)/shard_map/all_to_all | solution.py:21
  366.9 5.4 %shard_map.88 = bf16[1024,2048]{1,0:T(8,128)(2,1)} custom-call(bf16[1024,1024]{1,0:T(8,128)(2,1)} %select_convert_fusion.weights, bf16[1024,1024]{1,0:T(8,128)(2,1)} %bitcast.17.columns, bf16[1024,2048]{1,0:T(8,128)(2,1)} %shard_map.87.rest_0_), custom_call_target="tpu_custom_call", output_to_operand_aliasing={{}: (2, {})} | custom-call | flops 2147483648 | bytes 6291456 | tf_op jit(solution)/shard_map/pallas_call | solution.py:173
  372.3 6.0 %all-to-all-start.5 = ((bf16[64,16,2048]{2,1,0:T(8,128)(2,1)}), bf16[64,16,2048]{2,1,0:T(8,128)(2,1)}, u32[]{:S(2)}, u32[]{:S(2)}) async-start(bf16[64,16,2048]{2,1,0:T(8,128)(2,1)} %bitcast.56), calls=%async_computation.5 | async-start | bytes 8388608 | tf_op jit(solution)/shard_map/all_to_all | solution.py:21
  381.3 5.7 %collective-permute-start.10 = (bf16[1024,512]{1,0:T(8,128)(2,1)}, bf16[1024,512]{1,0:T(8,128)(2,1)}, u32[]{:S(2)}, u32[]{:S(2)}) collective-permute-start(bf16[1024,512]{1,0:T(8,128)(2,1)} %get-tuple-element.28), channel_id=1, source_target_pairs={{0,128},{1,129},{2,130},{3,131},{4,132},{5,133},{6,134},{7,135},{8... | collective-permute-start | bytes 3145736 | tf_op jit(solution)/shard_map/ppermute | solution.py:274
  396.4 11.9 %collective-permute-done.10 = bf16[1024,512]{1,0:T(8,128)(2,1)} collective-permute-done((bf16[1024,512]{1,0:T(8,128)(2,1)}, bf16[1024,512]{1,0:T(8,128)(2,1)}, u32[]{:S(2)}, u32[]{:S(2)}) %collective-permute-start.10) | collective-permute-done | bytes 1048608 | tf_op jit(solution)/shard_map/ppermute | solution.py:274
  412.8 17.9 %collective-permute-done.11 = bf16[1024,512]{1,0:T(8,128)(2,1)} collective-permute-done((bf16[1024,512]{1,0:T(8,128)(2,1)}, bf16[1024,512]{1,0:T(8,128)(2,1)}, u32[]{:S(2)}, u32[]{:S(2)}) %collective-permute-start.11) | collective-permute-done | bytes 1048608 | tf_op jit(solution)/shard_map/ppermute | solution.py:274
  445.3 5.5 %shard_map.89 = bf16[4,256,2048]{2,1,0:T(8,128)(2,1)} custom-call(bf16[1024,2048]{1,0:T(8,128)(2,1)} %select_dynamic-update-slice_fusion.2.rows_in), custom_call_target="tpu_custom_call" | custom-call | flops 1073741824 | bytes 8388608 | tf_op jit(solution)/shard_map/pallas_call | solution.py:76
  450.8 23.4 %all-to-all-done.5 = bf16[64,16,2048]{2,1,0:T(8,128)(2,1)} async-done(((bf16[64,16,2048]{2,1,0:T(8,128)(2,1)}), bf16[64,16,2048]{2,1,0:T(8,128)(2,1)}, u32[]{:S(2)}, u32[]{:S(2)}) %all-to-all-start.5) | async-done | bytes 4194336 | tf_op jit(solution)/shard_map/all_to_all | solution.py:21
  474.2 7.8 %shard_map.91 = bf16[1024,2048]{1,0:T(8,128)(2,1)} custom-call(bf16[4,256,256]{2,1,0:T(8,128)(2,1)} %bitcast.64, bf16[1024,2048]{1,0:T(8,128)(2,1)} %bitcast.26.columns, bf16[1024,2048]{1,0:T(8,128)(2,1)} %bitcast.62, f32[1,2048]{1,0:T(1,128)} %convert_element_type.62.gain), custom_call_target="tpu_custom_call" | custom-call | flops 2147483648 | bytes 12582912 | tf_op jit(solution)/shard_map/pallas_call | solution.py:104
  (110 shorter events, 108.4 us)
Async XLA Ops:
  0.6 42.0 %copy-start = (bf16[1,4,256,256]{3,2,1,0:T(8,128)(2,1)S(1)}, bf16[1,4,256,256]{3,2,1,0:T(8,128)(2,1)}, u32[]{:S(2)}) copy-start(bf16[1,4,256,256]{3,2,1,0:T(8,128)(2,1)} %param.9) | copy-start | bytes 1572868
  5.3 109.2 %all-to-all-start = ((bf16[64,16,2048]{2,1,0:T(8,128)(2,1)}), bf16[64,16,2048]{2,1,0:T(8,128)(2,1)}, u32[]{:S(2)}, u32[]{:S(2)}) async-start(bf16[64,16,2048]{2,1,0:T(8,128)(2,1)} %bitcast.61), calls=%async_computation | async-start | bytes 8388608 | tf_op jit(solution)/shard_map/all_to_all | solution.py:21
  18.6 10.5 %copy-start.17 = (bf16[1,4,256,256]{3,2,1,0:T(8,128)(2,1)S(1)}, bf16[1,4,256,256]{3,2,1,0:T(8,128)(2,1)}, u32[]{:S(2)}) copy-start(bf16[1,4,256,256]{3,2,1,0:T(8,128)(2,1)} %param.8) | copy-start | bytes 1572868
  21.3 49.1 %collective-permute-start = (bf16[1024,512]{1,0:T(8,128)(2,1)}, bf16[1024,512]{1,0:T(8,128)(2,1)S(1)}, u32[]{:S(2)}, u32[]{:S(2)}) collective-permute-start(bf16[1024,512]{1,0:T(8,128)(2,1)} %shard_map.78), channel_id=1, source_target_pairs={{0,192},{1,193},{2,194},{3,195},{4,196},{5,197},{6,198},{7,199},{8... | collective-permute-start | bytes 3145736 | tf_op jit(solution)/shard_map/ppermute | solution.py:234
  25.8 45.6 %collective-permute-start.1 = (bf16[1024,512]{1,0:T(8,128)(2,1)}, bf16[1024,512]{1,0:T(8,128)(2,1)}, u32[]{:S(2)}, u32[]{:S(2)}) collective-permute-start(bf16[1024,512]{1,0:T(8,128)(2,1)} %shard_map.78), channel_id=1, source_target_pairs={{64,192},{65,193},{66,194},{67,195},{68,196},{69,197},{70,198},{71... | collective-permute-start | bytes 3145736 | tf_op jit(solution)/shard_map/ppermute | solution.py:234
  27.4 45.0 %collective-permute-start.2 = (bf16[1024,512]{1,0:T(8,128)(2,1)}, bf16[1024,512]{1,0:T(8,128)(2,1)}, u32[]{:S(2)}, u32[]{:S(2)}) collective-permute-start(bf16[1024,512]{1,0:T(8,128)(2,1)} %shard_map.78), channel_id=1, source_target_pairs={{128,192},{129,193},{130,194},{131,195},{132,196},{133,197},{134,1... | collective-permute-start | bytes 3145736 | tf_op jit(solution)/shard_map/ppermute | solution.py:234
  120.3 57.1 %all-to-all-start.3 = ((bf16[64,16,1024]{2,1,0:T(8,128)(2,1)}), bf16[64,16,1024]{2,1,0:T(8,128)(2,1)}, u32[]{:S(2)}, u32[]{:S(2)}) async-start(bf16[64,16,1024]{2,1,0:T(8,128)(2,1)} %bitcast.66), calls=%async_computation.3 | async-start | bytes 4194304 | tf_op jit(solution)/shard_map/all_to_all | solution.py:21
  177.4 6.2 %copy-start.21 = (bf16[1,2048]{1,0:T(2,128)(2,1)S(1)}, bf16[1,2048]{1,0:T(2,128)(2,1)}, u32[]{:S(2)}) copy-start(bf16[1,2048]{1,0:T(2,128)(2,1)} %param.11) | copy-start | bytes 12292
  177.4 61.5 %all-to-all-start.1 = ((bf16[64,16,1024]{2,1,0:T(8,128)(2,1)}), bf16[64,16,1024]{2,1,0:T(8,128)(2,1)}, u32[]{:S(2)}, u32[]{:S(2)}) async-start(bf16[64,16,1024]{2,1,0:T(8,128)(2,1)} %bitcast.65), calls=%async_computation.1 | async-start | bytes 4194304 | tf_op jit(solution)/shard_map/all_to_all | solution.py:21
  188.1 40.6 %collective-permute-start.7 = (bf16[1024,512]{1,0:T(8,128)(2,1)}, bf16[1024,512]{1,0:T(8,128)(2,1)}, u32[]{:S(2)}, u32[]{:S(2)}) collective-permute-start(bf16[1024,512]{1,0:T(8,128)(2,1)} %add_convert_fusion), channel_id=1, source_target_pairs={{64,0},{128,64},{192,128},{65,1},{129,65},{193,129},{66,2},{130,66... | collective-permute-start | bytes 3145736 | tf_op jit(solution)/shard_map/ppermute | solution.py:254
  192.2 33.6 %collective-permute-start.8 = (bf16[1024,256]{1,0:T(8,128)(2,1)}, bf16[1024,256]{1,0:T(8,128)(2,1)}, u32[]{:S(2)}, u32[]{:S(2)}) collective-permute-start(bf16[1024,256]{1,0:T(8,128)(2,1)} %fusion.23), channel_id=1, source_target_pairs={{64,0},{128,64},{192,128},{65,1},{129,65},{193,129},{66,2},{130,66... | collective-permute-start | bytes 1572872 | tf_op jit(solution)/shard_map/ppermute | solution.py:254
  196.2 40.8 %collective-permute-start.6 = (bf16[1024,256]{1,0:T(8,128)(2,1)}, bf16[1024,256]{1,0:T(8,128)(2,1)}, u32[]{:S(2)}, u32[]{:S(2)}) collective-permute-start(bf16[1024,256]{1,0:T(8,128)(2,1)} %fusion.22), channel_id=1, source_target_pairs={{64,0},{128,64},{192,128},{65,1},{129,65},{193,129},{66,2},{130,66... | collective-permute-start | bytes 1572872 | tf_op jit(solution)/shard_map/ppermute | solution.py:254
  238.8 65.4 %all-to-all-start.4 = ((bf16[64,16,1024]{2,1,0:T(8,128)(2,1)}), bf16[64,16,1024]{2,1,0:T(8,128)(2,1)}, u32[]{:S(2)}, u32[]{:S(2)}) async-start(bf16[64,16,1024]{2,1,0:T(8,128)(2,1)} %bitcast.58), calls=%async_computation.4 | async-start | bytes 4194304 | tf_op jit(solution)/shard_map/all_to_all | solution.py:21
  254.0 38.4 %collective-permute-start.4 = (bf16[1024,512]{1,0:T(8,128)(2,1)S(1)}, bf16[1024,512]{1,0:T(8,128)(2,1)S(1)}, u32[]{:S(2)}, u32[]{:S(2)}) collective-permute-start(bf16[1024,512]{1,0:T(8,128)(2,1)S(1)} %add_convert_fusion.1), channel_id=1, source_target_pairs={{64,0},{128,64},{192,128},{65,1},{129,65},{193,129},{66,2},{130,66... | collective-permute-start | bytes 3145736 | tf_op jit(solution)/shard_map/ppermute | solution.py:254
  257.2 34.1 %collective-permute-start.5 = (bf16[1024,256]{1,0:T(8,128)(2,1)S(1)}, bf16[1024,256]{1,0:T(8,128)(2,1)S(1)}, u32[]{:S(2)}, u32[]{:S(2)}) collective-permute-start(bf16[1024,256]{1,0:T(8,128)(2,1)S(1)} %fusion.21), channel_id=1, source_target_pairs={{64,0},{128,64},{192,128},{65,1},{129,65},{193,129},{66,2},{130,66... | collective-permute-start | bytes 1572872 | tf_op jit(solution)/shard_map/ppermute | solution.py:254
  258.5 32.8 %copy-start.2 = (bf16[1024,256]{1,0:T(8,128)(2,1)S(1)}, bf16[1024,256]{1,0:T(8,128)(2,1)}, u32[]{:S(2)}) copy-start(bf16[1024,256]{1,0:T(8,128)(2,1)} %slice.150.here) | copy-start | bytes 1572868
  260.6 33.8 %copy-start.19 = (bf16[1024,256]{1,0:T(8,128)(2,1)}, bf16[1024,256]{1,0:T(8,128)(2,1)S(1)}, u32[]{:S(2)}) copy-start(bf16[1024,256]{1,0:T(8,128)(2,1)S(1)} %fusion.20) | copy-start | bytes 1572868
  260.6 41.9 %collective-permute-start.3 = (bf16[1024,256]{1,0:T(8,128)(2,1)S(1)}, bf16[1024,256]{1,0:T(8,128)(2,1)S(1)}, u32[]{:S(2)}, u32[]{:S(2)}) collective-permute-start(bf16[1024,256]{1,0:T(8,128)(2,1)S(1)} %fusion.20), channel_id=1, source_target_pairs={{64,0},{128,64},{192,128},{65,1},{129,65},{193,129},{66,2},{130,66... | collective-permute-start | bytes 1572872 | tf_op jit(solution)/shard_map/ppermute | solution.py:254
  304.2 62.7 %all-to-all-start.2 = ((bf16[64,16,1024]{2,1,0:T(8,128)(2,1)}), bf16[64,16,1024]{2,1,0:T(8,128)(2,1)}, u32[]{:S(2)}, u32[]{:S(2)}) async-start(bf16[64,16,1024]{2,1,0:T(8,128)(2,1)} %bitcast.57), calls=%async_computation.2 | async-start | bytes 4194304 | tf_op jit(solution)/shard_map/all_to_all | solution.py:21
  372.3 101.9 %all-to-all-start.5 = ((bf16[64,16,2048]{2,1,0:T(8,128)(2,1)}), bf16[64,16,2048]{2,1,0:T(8,128)(2,1)}, u32[]{:S(2)}, u32[]{:S(2)}) async-start(bf16[64,16,2048]{2,1,0:T(8,128)(2,1)} %bitcast.56), calls=%async_computation.5 | async-start | bytes 8388608 | tf_op jit(solution)/shard_map/all_to_all | solution.py:21
  381.3 26.9 %collective-permute-start.10 = (bf16[1024,512]{1,0:T(8,128)(2,1)}, bf16[1024,512]{1,0:T(8,128)(2,1)}, u32[]{:S(2)}, u32[]{:S(2)}) collective-permute-start(bf16[1024,512]{1,0:T(8,128)(2,1)} %get-tuple-element.28), channel_id=1, source_target_pairs={{0,128},{1,129},{2,130},{3,131},{4,132},{5,133},{6,134},{7,135},{8... | collective-permute-start | bytes 3145736 | tf_op jit(solution)/shard_map/ppermute | solution.py:274
  389.3 23.6 %collective-permute-start.9 = (bf16[1024,512]{1,0:T(8,128)(2,1)}, bf16[1024,512]{1,0:T(8,128)(2,1)}, u32[]{:S(2)}, u32[]{:S(2)}) collective-permute-start(bf16[1024,512]{1,0:T(8,128)(2,1)} %get-tuple-element.29), channel_id=1, source_target_pairs={{0,192},{1,193},{2,194},{3,195},{4,196},{5,197},{6,198},{7,199},{8... | collective-permute-start | bytes 3145736 | tf_op jit(solution)/shard_map/ppermute | solution.py:274
  391.5 39.2 %collective-permute-start.11 = (bf16[1024,512]{1,0:T(8,128)(2,1)}, bf16[1024,512]{1,0:T(8,128)(2,1)}, u32[]{:S(2)}, u32[]{:S(2)}) collective-permute-start(bf16[1024,512]{1,0:T(8,128)(2,1)} %pad_maximum_fusion.1), channel_id=1, source_target_pairs={{0,64},{1,65},{2,66},{3,67},{4,68},{5,69},{6,70},{7,71},{8,72},{9,... | collective-permute-start | bytes 3145736 | tf_op jit(solution)/shard_map/ppermute | solution.py:274
  474.2 7.8 %copy-start.1 = (bf16[1,4,256,256]{3,2,1,0:T(8,128)(2,1)S(1)}, bf16[1,4,256,256]{3,2,1,0:T(8,128)(2,1)}, u32[]{:S(2)}) copy-start(bf16[1,4,256,256]{3,2,1,0:T(8,128)(2,1)} %param.9) | copy-start | bytes 1572868
  (16 other events, 51.0 us)
